TPU v7x, 512 devices: a whole 4x8x8 slice. The times are simulated.
512 devices in a mesh: px: 32 (over x, z_hi, core), lt: 16 (over y, z_lo).
Axes of the slice: x: 4, y: 8, z: 8 (z_hi: 4, z_lo: 2; z = z_hi * 2 + z_lo), core: 2. Of those that a mesh axis runs over, the one named last changes fastest.
Arguments:
- observed: bfloat16 [3, 512, 262144], P(None, 'lt', 'px'), may hold values from 0 to 1
- shadow: int32 [512, 262144], P('lt', 'px'), may hold values from 0 to 1, as said below
- view_ids: int32 [262144], P('px'), may hold values from 0 to 15
- surface_points: float32 [3, 262144], P(None, 'px'), may hold values from -1 to 1
- frame_coords: float32 [2, 262144], P(None, 'px'), may hold values from 0 to 1
- pixel_params: float32 [12, 262144], P(None, 'px'), may hold values from -3.1416 to 3.1416, as said below
- light_power: float32 [3, 512], P(None, 'lt'), may hold values from 4 to 40
- light_pos: float32 [3, 512], P(None, 'lt'), may hold values from -6 to 6, as said below
- camera_pos: float32 [3, 16], replicated, may hold values from -7 to 7, as said below
Outputs:
- new_params: float32 [12, 262144], P(None, 'px')
- new_power: float32 [3, 512], P(None, 'lt')
- new_light_pos: float32 [3, 512], P(None, 'lt')
- loss: float32 [], replicated
Inputs may be any that keep to these rules, and one draw needn't show every extreme that they name: `shadow`: 1 where the light reaches the pixel, 0 elsewhere. `pixel_params`: rows 0 to 2 diffuse albedo in 0.05 to 0.9, rows 3 to 5 specular albedo in 0.05 to 1, rows 6 and 7 logarithms of the two roughnesses in -2.5 to -0.7, rows 8 and 9 normal tilts in -0.4 to 0.4, row 10 an angle in -pi to pi, row 11 reflectance at normal incidence in 0.02 to 0.3. `light_pos`: each light lies 4 to 6 from the anchor, at most 1 radian from the third axis. `camera_pos`: each camera lies 5 to 7 from the anchor, at most 0.8 radian from the third axis.
All inputs are finite; a program needn't handle non-finite values.
Results may differ from a plain program's by a relative error of at most 0.0003.
Values sent between devices are 32-bit elements; how exact they have to be, the bound alone decides.
No kernel may reach another device: no remote copies, remote signals or barrier semaphores. Data moves between devices by JAX's collectives and lax.ppermute only.
A program may use at most 64 MiB of HBM per device.

v0:
```python
import functools
import math

import jax
import jax.numpy as jnp
from jax import lax
from jax.sharding import Mesh
from jax.sharding import PartitionSpec as P

PX = ("px_0", "px_1", "px_2")
LT = ("lt_0", "lt_1")
PX_LT = ("px_0", "px_1", "px_2", "lt_0", "lt_1")


softness = 0.01
epsilon = 1e-06
stride = 0.2


def cut_along(x, dim, count):
    lengths = x.shape
    parts = x.reshape(*lengths[:dim], count, lengths[dim] // count, *lengths[dim + 1 :])
    return jnp.moveaxis(parts, dim, 0)


def summed_on_arrival(x, axis, dim):
    parts = cut_along(x, dim, lax.axis_size(axis))
    arrived = lax.all_to_all(parts, axis, split_axis=0, concat_axis=0, tiled=True)
    return arrived.sum(axis=0)


def over_axes(x, axes):
    return functools.reduce(lax.psum, axes, x)


def in_order(parts, dim):
    lengths = list(parts.shape[1:])
    lengths[dim] *= parts.shape[0]
    return jnp.moveaxis(parts, 0, dim).reshape(lengths)


def from_everyone(x, axis):
    count = lax.axis_size(axis)
    return lax.all_to_all(jnp.broadcast_to(x[None], (count, *x.shape)), axis, 0, 0, tiled=True)


def collect(x, axis, dim):
    return in_order(from_everyone(x, axis), dim)


def inner_three(first, second):
    return first[0] * second[0] + first[1] * second[1] + first[2] * second[2]


def cross_three(first, second):
    return [
        first[1] * second[2] - first[2] * second[1],
        first[2] * second[0] - first[0] * second[2],
        first[0] * second[1] - first[1] * second[0],
    ]


def soft_cosine(value):
    return 0.5 * (value + jnp.sqrt(value * value + softness))


def shade(params, points, frames, cameras, light_power, light_pos, visible, observed):
    polar_angle = frames[0]
    azimuth = 2.0 * math.pi * frames[1]
    cos_polar, sin_polar = (jnp.cos(polar_angle), jnp.sin(polar_angle))
    cos_azimuth, sin_azimuth = (jnp.cos(azimuth), jnp.sin(azimuth))
    base_normal = [sin_polar * cos_azimuth, sin_polar * sin_azimuth, cos_polar]
    base_tangent = [cos_polar * cos_azimuth, cos_polar * sin_azimuth, -sin_polar]
    base_bitangent = [-sin_azimuth, cos_azimuth, jnp.zeros_like(cos_azimuth)]
    tilt_u, tilt_v = (params[8], params[9])
    scaled = lax.rsqrt(1.0 + tilt_u * tilt_u + tilt_v * tilt_v)
    normal = [
        (base_normal[coord] + tilt_u * base_tangent[coord] + tilt_v * base_bitangent[coord])
        * scaled
        for coord in range(3)
    ]
    spin_angle = params[10]
    turned = [
        jnp.cos(spin_angle) * base_tangent[coord] + jnp.sin(spin_angle) * base_bitangent[coord]
        for coord in range(3)
    ]
    along_normal = inner_three(turned, normal)
    raw_tangent = [turned[coord] - along_normal * normal[coord] for coord in range(3)]
    inv_length = lax.rsqrt(inner_three(raw_tangent, raw_tangent))
    tangent = [raw_tangent[coord] * inv_length for coord in range(3)]
    bitangent = cross_three(normal, tangent)
    toward = [cameras[coord] - points[coord] for coord in range(3)]
    view_scale = lax.rsqrt(inner_three(toward, toward))
    view_dir = [toward[coord] * view_scale for coord in range(3)]
    light_offset = [light_pos[coord][:, None] - points[coord][None, :] for coord in range(3)]
    distance_sq = inner_three(light_offset, light_offset)
    light_scale = lax.rsqrt(distance_sq)
    light_dir = [light_offset[coord] * light_scale for coord in range(3)]
    halfway = [light_dir[coord] + view_dir[coord][None, :] for coord in range(3)]
    half_scale = lax.rsqrt(inner_three(halfway, halfway))
    half_dir = [halfway[coord] * half_scale for coord in range(3)]
    alpha_u = jnp.exp(params[6])
    alpha_v = jnp.exp(params[7])
    fresnel_zero = params[11]

    def smith_lambda(direction):
        along = inner_three(direction, tangent)
        across = inner_three(direction, bitangent)
        lifted = soft_cosine(inner_three(direction, normal))
        ratio = (alpha_u * alpha_u * along * along + alpha_v * alpha_v * across * across) / (
            lifted * lifted
        )
        return 0.5 * (jnp.sqrt(1.0 + ratio) - 1.0)

    half_along = inner_three(half_dir, tangent) / alpha_u
    half_across = inner_three(half_dir, bitangent) / alpha_v
    half_normal = inner_three(half_dir, normal)
    quadric = half_along * half_along + half_across * half_across + half_normal * half_normal
    microfacet = 1.0 / (math.pi * alpha_u * alpha_v * quadric * quadric)
    shadowing = 1.0 / ((1.0 + smith_lambda(light_dir)) * (1.0 + smith_lambda(view_dir)))
    cos_view_half = inner_three(view_dir, half_dir)
    fresnel = fresnel_zero + (1.0 - fresnel_zero) * (1.0 - cos_view_half) ** 5
    glossy = microfacet * shadowing * fresnel / (4.0 * soft_cosine(inner_three(view_dir, normal)))
    diffuse_term = soft_cosine(inner_three(light_dir, normal)) / math.pi
    energy = jnp.zeros((), params.dtype)
    for channel in range(3):
        reflected = (params[channel] * diffuse_term + params[3 + channel] * glossy) / distance_sq
        residual = visible * (light_power[channel][:, None] * reflected - observed[channel])
        energy = energy + 0.5 * jnp.sum(residual * residual)
    return energy


def shards(
    observed,
    shadow,
    view_ids,
    surface_points,
    frame_coords,
    pixel_params,
    light_power,
    light_pos,
    camera_pos,
):
    pixel_count = pixel_params.shape[1]
    block_size = min(pixel_count, 2048)
    block_total = pixel_count // block_size
    view_count = camera_pos.shape[1]
    view_range = jnp.arange(view_count, dtype=jnp.int32)

    def accumulate(block_index, carry):
        grad_params, power_sum, pos_sum, energy_sum = carry
        offset = block_index * block_size

        def window(array):
            return lax.dynamic_slice_in_dim(array, offset, block_size, array.ndim - 1)

        view_index = window(view_ids)
        onehot = (view_index[None, :] == view_range[:, None]).astype(jnp.float32)
        cameras = jnp.dot(camera_pos, onehot, precision=lax.Precision.HIGHEST)
        points = window(surface_points)
        frames = window(frame_coords)
        visible = window(shadow).astype(jnp.float32)
        measured = window(observed).astype(jnp.float32)

        def energy_of(params, power, positions):
            return shade(params, points, frames, cameras, power, positions, visible, measured)

        energy, pullback = jax.vjp(energy_of, window(pixel_params), light_power, light_pos)
        grad_block, grad_power, grad_pos = pullback(jnp.ones_like(energy))
        grad_params = lax.dynamic_update_slice_in_dim(grad_params, grad_block, offset, 1)
        return (grad_params, power_sum + grad_power, pos_sum + grad_pos, energy_sum + energy)

    start_carry = (
        jnp.zeros_like(pixel_params),
        jnp.zeros_like(light_power),
        jnp.zeros_like(light_pos),
        jnp.zeros((), jnp.float32),
    )
    grad_params, grad_power, grad_pos, energy_sum = lax.fori_loop(
        0, block_total, accumulate, start_carry
    )
    local_squares = 2.0 * energy_sum
    pixel_total = pixel_count * lax.axis_size(PX)
    light_total = light_power.shape[1] * lax.axis_size(LT)
    share_size = pixel_count // lax.axis_size(LT)
    grad_share = summed_on_arrival(grad_params, LT, 1)
    pixel_sq = jnp.sum(grad_share * grad_share)
    power_full, pos_full = (over_axes(grad_power, PX), over_axes(grad_pos, PX))
    light_sq = jnp.sum(power_full * power_full) + jnp.sum(pos_full * pos_full)
    pixel_norm, light_norm, squares_total = (
        over_axes(pixel_sq, PX_LT),
        over_axes(light_sq / lax.axis_size(PX), PX_LT),
        over_axes(local_squares, PX_LT),
    )
    pixel_scale = jnp.sqrt(pixel_norm / (12 * pixel_total) + epsilon)
    light_scale = jnp.sqrt(light_norm / (6 * light_total) + epsilon)
    own_params = lax.dynamic_slice_in_dim(
        pixel_params, lax.axis_index(LT) * share_size, share_size, 1
    )
    stepped = own_params - stride * grad_share / pixel_scale
    new_params = collect(stepped, LT, 1)
    new_power = light_power - stride * power_full / light_scale
    new_light_pos = light_pos - stride * pos_full / light_scale
    loss = squares_total / (3 * light_total * pixel_total)
    return (new_params, new_power, new_light_pos, loss)


def solution(mesh):
    torus = Mesh(mesh.devices.reshape(4, 4, 2, 8, 2), ("px_0", "px_1", "px_2", "lt_0", "lt_1"))
    placed = (
        P(None, LT, PX),
        P(LT, PX),
        P(PX),
        P(None, PX),
        P(None, PX),
        P(None, PX),
        P(None, LT),
        P(None, LT),
        P(),
    )
    return jax.shard_map(
        shards,
        mesh=torus,
        in_specs=placed,
        out_specs=(P(None, PX), P(None, LT), P(None, LT), P()),
        check_vma=False,
    )
```

profile of v0, /device:TPU:2, one launch (start us, length us, event | category | flops | bytes accessed | tf_op | source)
XLA Modules:
  0.0 270.4 jit_solution(11057672612064473127)
XLA Ops:
  0.7 157.4 %while.23 = (s32[]{:T(128)}, f32[12,8192]{1,0:T(8,128)S(1)}, f32[3,32]{1,0:T(4,128)S(1)}, f32[3,32]{1,0:T(4,128)S(1)}, f32[]{:T(128)}, /*index=5*/f32[3,32]{1,0:...) while((s32[]{:T(128)}, f32[12,8192]{1,0:T(8,128)S(1)}, ...), condition=%wide.region_46.47_spmd.clone, body=%wide.region_0.46_spmd.clone.sunk | while | flops 115552848 | bytes 32035720 | solution.py:179
  4.9 1.7 broadcast_divide_fusion.12
  6.5 2.2 broadcast_subtract_fusion.2
  9.9 1.9 multiply_reduce_fusion.64
  11.8 1.3 multiply_reduce_fusion.65
  13.1 1.8 multiply_reduce_fusion.61
  15.0 1.8 multiply_reduce_fusion.58
  18.8 1.3 multiply_reduce_fusion.62
  20.1 1.3 multiply_reduce_fusion.59
  27.2 1.6 multiply_reduce_fusion.68
  31.5 2.6 fusion.85
  35.3 1.7 multiply_add_fusion.68
  37.0 1.4 add_add_fusion.33
  38.4 1.4 add_add_fusion.34
  44.2 1.7 broadcast_divide_fusion.12
  45.9 2.2 broadcast_subtract_fusion.2
  49.2 1.9 multiply_reduce_fusion.64
  51.1 1.3 multiply_reduce_fusion.65
  52.4 1.8 multiply_reduce_fusion.61
  54.3 1.8 multiply_reduce_fusion.58
  58.1 1.3 multiply_reduce_fusion.62
  59.4 1.3 multiply_reduce_fusion.59
  66.5 1.6 multiply_reduce_fusion.68
  70.8 2.6 fusion.85
  74.6 1.7 multiply_add_fusion.68
  76.3 1.4 add_add_fusion.33
  77.7 1.4 add_add_fusion.34
  83.5 1.7 broadcast_divide_fusion.12
  85.2 2.3 broadcast_subtract_fusion.2
  88.5 1.9 multiply_reduce_fusion.64
  90.5 1.3 multiply_reduce_fusion.65
  91.8 1.8 multiply_reduce_fusion.61
  93.6 1.8 multiply_reduce_fusion.58
  97.4 1.3 multiply_reduce_fusion.62
  98.7 1.3 multiply_reduce_fusion.59
  105.8 1.6 multiply_reduce_fusion.68
  110.1 2.6 fusion.85
  114.0 1.7 multiply_add_fusion.68
  115.7 1.4 add_add_fusion.33
  117.1 1.4 add_add_fusion.34
  122.8 1.7 broadcast_divide_fusion.12
  124.5 2.2 broadcast_subtract_fusion.2
  127.8 1.9 multiply_reduce_fusion.64
  129.8 1.3 multiply_reduce_fusion.65
  131.1 1.8 multiply_reduce_fusion.61
  132.9 1.8 multiply_reduce_fusion.58
  136.7 1.3 multiply_reduce_fusion.62
  138.0 1.3 multiply_reduce_fusion.59
  145.1 1.6 multiply_reduce_fusion.68
  149.4 2.6 fusion.85
  153.3 1.7 multiply_add_fusion.68
  155.0 1.4 add_add_fusion.33
  156.4 1.4 add_add_fusion.34
  159.5 9.1 %all-to-all-start = ((f32[16,12,512]{2,1,0:T(8,128)}), f32[16,12,512]{2,1,0:T(8,128)S(1)}, u32[]{:S(2)}, u32[]{:S(2)}) async-start(f32[16,12,512]{2,1,0:T(8,128)} %copy.13), calls=%async_computation | async-start | bytes 1048576 | tf_op jit(solution)/shard_map/all_to_all | solution.py:28
  168.7 8.6 %all-reduce.22 = (f32[3,32]{1,0:T(4,128)S(1)}, f32[3,32]{1,0:T(4,128)S(1)}) all-reduce(f32[3,32]{1,0:T(4,128)S(1)} %get-tuple-element.409, f32[3,32]{1,0:T(4,128)S(1)} %get-tuple-element.410), channel_id=1, replica_groups=mesh['px_0'=4,'px_1'=4,'px_2'=2,'lt_0'=8,'lt_1'=2] {'px_0'}, use_global_device_ids=true, to_apply=%region_54.55 | all-reduce | flops 192 | bytes 1536 | tf_op jit(solution)/shard_map/psum | solution.py:33
  177.3 16.7 %all-reduce.20 = (f32[3,32]{1,0:T(4,128)S(1)}, f32[3,32]{1,0:T(4,128)S(1)}) all-reduce(f32[3,32]{1,0:T(4,128)S(1)} %get-tuple-element.554, f32[3,32]{1,0:T(4,128)S(1)} %get-tuple-element.555), channel_id=1, replica_groups=mesh['px_0'=4,'px_1'=4,'px_2'=2,'lt_0'=8,'lt_1'=2] {'px_1'}, use_global_device_ids=true, to_apply=%region_55.56 | all-reduce | flops 192 | bytes 1536 | tf_op jit(solution)/shard_map/psum | solution.py:33
  194.0 2.5 all-reduce.25
  199.7 10.8 %all-reduce.21 = (f32[]{:T(128)}, f32[]{:T(128)}, f32[]{:T(128)}) all-reduce(f32[]{:T(128)} %multiply_reduce_fusion.41, f32[]{:T(128)S(6)} %div.570, f32[]{:T(128)S(6)} %mul_shard_map.3), channel_id=1, replica_groups=mesh['px_0'=4,'px_1'=4,'px_2'=2,'lt_0'=8,'lt_1'=2] {'px_0'}, use_global_device_ids=true, to_apply=%region_49.50 | all-reduce | flops 3 | bytes 24 | tf_op jit(solution)/shard_map/psum | solution.py:33
  210.4 9.8 %all-reduce.19 = (f32[]{:T(128)}, f32[]{:T(128)}, f32[]{:T(128)}) all-reduce(f32[]{:T(128)} %get-tuple-element.551, f32[]{:T(128)} %get-tuple-element.552, f32[]{:T(128)} %get-tuple-element.553), channel_id=1, replica_groups=mesh['px_0'=4,'px_1'=4,'px_2'=2,'lt_0'=8,'lt_1'=2] {'px_1'}, use_global_device_ids=true, to_apply=%region_50.51 | all-reduce | flops 3 | bytes 24 | tf_op jit(solution)/shard_map/psum | solution.py:33
  220.2 3.1 %all-reduce.24 = (f32[]{:T(128)}, f32[]{:T(128)}, f32[]{:T(128)}) all-reduce(f32[]{:T(128)} %get-tuple-element.546, f32[]{:T(128)} %get-tuple-element.547, f32[]{:T(128)} %get-tuple-element.548), channel_id=1, replica_groups=mesh['px_0'=4,'px_1'=4,'px_2'=2,'lt_0'=8,'lt_1'=2] {'px_2'}, use_global_device_ids=true, to_apply=%region_51.52 | all-reduce | flops 3 | bytes 24 | tf_op jit(solution)/shard_map/psum | solution.py:33
  223.3 18.0 %all-reduce.18 = (f32[]{:T(128)}, f32[]{:T(128)}, f32[]{:T(128)}) all-reduce(f32[]{:T(128)} %get-tuple-element.559, f32[]{:T(128)} %get-tuple-element.560, f32[]{:T(128)} %get-tuple-element.561), channel_id=1, replica_groups=mesh['px_0'=4,'px_1'=4,'px_2'=2,'lt_0'=8,'lt_1'=2] {'lt_0'}, use_global_device_ids=true, to_apply=%region_52.53 | all-reduce | flops 3 | bytes 24 | tf_op jit(solution)/shard_map/psum | solution.py:33
  241.3 5.5 %all-reduce.23 = (f32[]{:T(128)}, f32[]{:T(128)}, f32[]{:T(128)}) all-reduce(f32[]{:T(128)} %get-tuple-element.543, f32[]{:T(128)} %get-tuple-element.544, f32[]{:T(128)} %get-tuple-element.545), channel_id=1, replica_groups=mesh['px_0'=4,'px_1'=4,'px_2'=2,'lt_0'=8,'lt_1'=2] {'lt_1'}, use_global_device_ids=true, to_apply=%region_53.54 | all-reduce | flops 3 | bytes 24 | tf_op jit(solution)/shard_map/psum | solution.py:33
  249.2 5.6 %all-to-all-start.1 = ((f32[16,12,512]{2,1,0:T(8,128)}), f32[16,12,512]{2,1,0:T(8,128)S(1)}, u32[]{:S(2)}, u32[]{:S(2)}) async-start(f32[16,12,512]{2,1,0:T(8,128)} %broadcast_in_dim.232), calls=%async_computation.1 | async-start | bytes 1048576 | tf_op jit(solution)/shard_map/all_to_all | solution.py:44
  256.7 11.2 %all-to-all-done.1 = f32[16,12,512]{2,1,0:T(8,128)S(1)} async-done(((f32[16,12,512]{2,1,0:T(8,128)}), f32[16,12,512]{2,1,0:T(8,128)S(1)}, u32[]{:S(2)}, u32[]{:S(2)}) %all-to-all-start.1) | async-done | bytes 393248 | tf_op jit(solution)/shard_map/all_to_all | solution.py:44
  (149 shorter events, 67.0 us)
Async XLA Ops:
  0.7 9.2 %copy-start = (s32[32,8192]{1,0:T(8,128)S(1)}, s32[32,8192]{1,0:T(8,128)}, u32[]{:S(2)}) copy-start(s32[32,8192]{1,0:T(8,128)} %get-tuple-element.1179) | copy-start | bytes 3145732 | tf_op jit(solution)/shard_map/while
  34.0 1.3 copy-start.1
  40.0 9.2 %copy-start = (s32[32,8192]{1,0:T(8,128)S(1)}, s32[32,8192]{1,0:T(8,128)}, u32[]{:S(2)}) copy-start(s32[32,8192]{1,0:T(8,128)} %get-tuple-element.1179) | copy-start | bytes 3145732 | tf_op jit(solution)/shard_map/while
  73.3 1.3 copy-start.1
  79.3 9.2 %copy-start = (s32[32,8192]{1,0:T(8,128)S(1)}, s32[32,8192]{1,0:T(8,128)}, u32[]{:S(2)}) copy-start(s32[32,8192]{1,0:T(8,128)} %get-tuple-element.1179) | copy-start | bytes 3145732 | tf_op jit(solution)/shard_map/while
  112.7 1.3 copy-start.1
  118.7 9.2 %copy-start = (s32[32,8192]{1,0:T(8,128)S(1)}, s32[32,8192]{1,0:T(8,128)}, u32[]{:S(2)}) copy-start(s32[32,8192]{1,0:T(8,128)} %get-tuple-element.1179) | copy-start | bytes 3145732 | tf_op jit(solution)/shard_map/while
  152.0 1.3 copy-start.1
  159.5 96.6 %copy-start.2 = (f32[3,32]{1,0:T(4,128)S(1)}, f32[3,32]{1,0:T(4,128)}, u32[]{:S(2)}) copy-start(f32[3,32]{1,0:T(4,128)} %get-tuple-element.1206) | copy-start | bytes 1156
  159.5 96.6 %copy-start.3 = (f32[3,32]{1,0:T(4,128)S(1)}, f32[3,32]{1,0:T(4,128)}, u32[]{:S(2)}) copy-start(f32[3,32]{1,0:T(4,128)} %get-tuple-element.1207) | copy-start | bytes 1156
  159.5 39.5 %all-to-all-start = ((f32[16,12,512]{2,1,0:T(8,128)}), f32[16,12,512]{2,1,0:T(8,128)S(1)}, u32[]{:S(2)}, u32[]{:S(2)}) async-start(f32[16,12,512]{2,1,0:T(8,128)} %copy.13), calls=%async_computation | async-start | bytes 1048576 | tf_op jit(solution)/shard_map/all_to_all | solution.py:28
  249.2 18.7 %all-to-all-start.1 = ((f32[16,12,512]{2,1,0:T(8,128)}), f32[16,12,512]{2,1,0:T(8,128)S(1)}, u32[]{:S(2)}, u32[]{:S(2)}) async-start(f32[16,12,512]{2,1,0:T(8,128)} %broadcast_in_dim.232), calls=%async_computation.1 | async-start | bytes 1048576 | tf_op jit(solution)/shard_map/all_to_all | solution.py:44
where the time goes:
time: 273 us; the launch traced here: 270 us
  other arithmetic  139 us (51%)
  blocking collectives  75 us (27%)
  starting transfers between devices  14.7 us (5%)
  local copies, waits for them, and re-layouts  12.9 us (5%)
  waiting for transfers between devices  11.2 us (4%)
  loops' own time  9.04 us (3%)
  between operations  5.21 us (2%)
  matrix products  3.35 us (1%)
    psum x8, blocking collectives, over_axes(): return functools.reduce(lax.psum, axes, x)  75 us
    reduce_sum x12, other arithmetic, shade(): energy = energy + 0.5 * jnp.sum(residual * residual)  22.4 us
    reduce_sum x12, other arithmetic, shade(): light_power[channel][:, None] * reflected - observed[channel]  15.7 us
    reduce_sum x12, other arithmetic, shade(): params[3 + channel] * glossy  13.8 us
    all_to_all x1, waiting for transfers between devices, from_everyone(): lax.all_to_all(jnp.broadcast_to(x[None], (count, *x.shape)), axis, 0, 0,...  11.2 us
    add_any x8, other arithmetic, shade(): scaled = lax.rsqrt(1.0 + tilt_u * tilt_u + tilt_v * tilt_v)  11.2 us
    add_any x4, other arithmetic, shade(): light_scale = lax.rsqrt(distance_sq)  10.3 us
    all_to_all x1, starting transfers between devices, summed_on_arrival(): lax.all_to_all(parts, axis, split_axis=0, concat_axis=0, tiled=True)  9.14 us
  transfers between devices with their start and end apart: 2, of which 1 were waited for; matrix products, arithmetic and copies ran while one was open for 1% of the time, Pallas kernels for 0%

commit v1 on v0

v1 whole, which is shorter than its diff:
```python
import functools
import math

import jax
import jax.numpy as jnp
from jax import lax
from jax.experimental import pallas as pl
from jax.experimental.pallas import tpu as pltpu
from jax.sharding import Mesh
from jax.sharding import PartitionSpec as P

PX = ("px_0", "px_1", "px_2")
LT = ("lt_0", "lt_1")

SOFT = 0.01
EPS = 1e-06
STRIDE = 0.2
LANES = 128
SUBS = 8
ROWS = 12
BLOCK = 1024
CHUNKS = BLOCK // LANES
RAW = 24
GROUP = 1

(TX, TY, TZ, BX, BY, BZ, NX, NY, NZ, PT, PB, PN, VT, VB, VN, AX2, AY2, IX2, IY2, KG, F0, F1, K5,
 KD0, KD1, KD2, KS0, KS1, KS2) = range(29)
TABLE = 29
(SD0, SD1, SD2, SS0, SS1, SS2, SF, SH, V11, V22, V12, V13, V23, U11, U22, U12, U13, U23, WT, WB) = range(20)
SUMS = 20


def inner_three(first, second):
    return first[0] * second[0] + first[1] * second[1] + first[2] * second[2]


def pixel_frame(row, ids, camera_ref):
    azimuth = 2.0 * math.pi * row(17)
    ca, sa = jnp.cos(row(16)), jnp.sin(row(16))
    cz, sz = jnp.cos(azimuth), jnp.sin(azimuth)
    base_n = [sa * cz, sa * sz, ca]
    base_t = [ca * cz, ca * sz, -sa]
    base_b = [-sz, cz]
    u, v, spin = row(8), row(9), row(10)
    cs, sn = jnp.cos(spin), jnp.sin(spin)
    kappa = lax.rsqrt(1.0 + u * u + v * v)
    along = kappa * (u * cs + v * sn)
    inv = lax.rsqrt(1.0 - along * along)
    n_loc = [kappa, kappa * u, kappa * v]
    t_loc = [-along * n_loc[0] * inv, (cs - along * n_loc[1]) * inv, (sn - along * n_loc[2]) * inv]
    kb = kappa * inv
    b_loc = [kb * (u * sn - v * cs), -kb * sn, kb * cs]

    def world(loc):
        return [
            loc[0] * base_n[0] + loc[1] * base_t[0] + loc[2] * base_b[0],
            loc[0] * base_n[1] + loc[1] * base_t[1] + loc[2] * base_b[1],
            loc[0] * base_n[2] + loc[1] * base_t[2],
        ]

    tangent, bitangent, normal = world(t_loc), world(b_loc), world(n_loc)
    point = [row(12), row(13), row(14)]
    camera = [jnp.full_like(u, camera_ref[c, 0]) for c in range(3)]
    for view in range(1, camera_ref.shape[1]):
        chosen = ids == view
        camera = [jnp.where(chosen, camera_ref[c, view], camera[c]) for c in range(3)]
    toward = [camera[c] - point[c] for c in range(3)]
    scale = lax.rsqrt(inner_three(toward, toward))
    view_dir = [toward[c] * scale for c in range(3)]
    vt, vb, vn = (inner_three(view_dir, f) for f in (tangent, bitangent, normal))
    ax, ay = jnp.exp(row(6)), jnp.exp(row(7))
    ax2, ay2 = ax * ax, ay * ay
    ix2, iy2 = 1.0 / ax2, 1.0 / ay2
    vroot = lax.rsqrt(vn * vn + SOFT)
    cv = 0.5 * (vn + (vn * vn + SOFT) * vroot)
    wv2 = cv * cv + ax2 * vt * vt + ay2 * vb * vb
    rwv = lax.rsqrt(wv2)
    rcv = 1.0 / (cv + wv2 * rwv)
    return dict(
        tangent=tangent, bitangent=bitangent, normal=normal, point=point,
        vt=vt, vb=vb, vn=vn, ax=ax, ay=ay, ax2=ax2, ay2=ay2, ix2=ix2, iy2=iy2,
        vroot=vroot, cv=cv, rwv=rwv, rcv=rcv, kappa=kappa, inv=inv, along=along,
        t_loc=t_loc, b_loc=b_loc,
    )


def pair_terms(px, light, visible, measured):
    lx, ly, lz, pw = light[0], light[1], light[2], light[3:6]
    ot = lx * px(TX) + ly * px(TY) + lz * px(TZ) - px(PT)
    ob = lx * px(BX) + ly * px(BY) + lz * px(BZ) - px(PB)
    on = lx * px(NX) + ly * px(NY) + lz * px(NZ) - px(PN)
    r = lax.rsqrt(ot * ot + ob * ob + on * on)
    id2 = r * r
    lt, lb, ln = ot * r, ob * r, on * r
    m = (lt * px(VT) + lb * px(VB)) + (ln * px(VN) + 1.0)
    a1, a2, a3 = lt + px(VT), lb + px(VB), ln + px(VN)
    b1, b2 = a1 * px(IX2), a2 * px(IY2)
    rq = lax.rsqrt(b1 * a1 + b2 * a2 + a3 * a3)
    rq = rq * rq
    rm = lax.rsqrt(m)
    om = 1.0 - (m * rm) * math.sqrt(0.5)
    om2 = om * om
    om4 = om2 * om2
    s5 = om4 * om
    fresnel = px(F0) + px(F1) * s5
    lsq = ln * ln + SOFT
    rs = lax.rsqrt(lsq)
    cn = 0.5 * (ln + lsq * rs)
    xt, xb = lt * px(AX2), lb * px(AY2)
    wsq = cn * cn + (xt * lt + xb * lb)
    rw = lax.rsqrt(wsq)
    rc = lax.rsqrt(cn + wsq * rw)
    rc = rc * rc
    cni = cn * id2
    mq = m * rq
    bi = (mq * mq) * (rc * cni) * px(KG)
    gi = bi * fresnel
    squares = None
    power_terms = []
    ys = []
    for c in range(3):
        refl = px(KD0 + c) * cni + px(KS0 + c) * gi
        res = visible * (pw[c] * refl - measured[c])
        squares = res * res if c == 0 else squares + res * res
        power_terms.append(res * refl)
        ys.append(res * pw[c])
    dcn = ys[0] * px(KD0) + ys[1] * px(KD1) + ys[2] * px(KD2)
    dgl = ys[0] * px(KS0) + ys[1] * px(KS1) + ys[2] * px(KS2)
    h = gi * dgl
    s = cni * dcn + h
    x = dgl * bi
    mm = rm * (2.0 * (h * rm) - (x * om4) * px(K5))
    hw = h * rw
    uu = hw * rc
    ww = rs * (s - hw * cn)
    v4 = (4.0 * h) * rq
    v1, v2, v3 = v4 * a1, v4 * a2, v4 * a3
    u1, u2 = uu * lt, uu * lb
    sums = [None] * SUMS
    for c in range(3):
        sums[SD0 + c] = ys[c] * cni
        sums[SS0 + c] = ys[c] * gi
    sums[SF] = x - x * s5
    sums[SH] = h
    sums[V11], sums[V22], sums[V12] = v1 * a1, v2 * a2, v1 * a2
    sums[V13], sums[V23] = v1 * a3, v2 * a3
    sums[U11], sums[U22], sums[U12] = u1 * lt, u2 * lb, u1 * lb
    sums[U13], sums[U23] = u1 * ln, u2 * ln
    sums[WT], sums[WB] = ww * lt, ww * lb
    gt = mm * px(VT) - uu * xt - v4 * b1
    gb = mm * px(VB) - uu * xb - v4 * b2
    gn = mm * px(VN) + ww - v3
    radial = lt * gt + lb * gb + ln * gn + 2.0 * s
    gt, gb, gn = (gt - lt * radial) * r, (gb - lb * radial) * r, (gn - ln * radial) * r
    light_terms = power_terms + [
        gt * px(TX + c) + gb * px(BX + c) + gn * px(NX + c) for c in range(3)
    ]
    return sums, light_terms, squares


def fold(x):
    total = x[:SUBS]
    for g in range(1, x.shape[0] // SUBS):
        total = total + x[g * SUBS : (g + 1) * SUBS]
    return total


def gradient_kernel(
    camera_ref, observed_ref, shadow_ref, ids_ref, points_ref, frames_ref, params_ref, power_ref, pos_ref,
    grads_ref, light_ref,
    raw, table, sums_ref, light_wide, light_sum, square_sum,
):
    step = pl.program_id(0)
    lights = shadow_ref.shape[0]
    groups = lights // SUBS
    lane = lax.broadcasted_iota(jnp.int32, (SUBS, lights), 1)
    sub = lax.broadcasted_iota(jnp.int32, (SUBS, lights), 0)

    @pl.when(step == 0)
    def _():
        light_sum[...] = jnp.zeros_like(light_sum)
        square_sum[...] = jnp.zeros_like(square_sum)
        for q in range(6):
            source = pos_ref if q < 3 else power_ref
            values = source[q % 3 : q % 3 + 1, :]
            for g in range(groups):
                picked = jnp.where(lane == sub + g * SUBS, values, 0.0)
                column = jnp.sum(picked, axis=1, keepdims=True)
                light_wide[q, g * SUBS : (g + 1) * SUBS, :] = jnp.broadcast_to(column, (SUBS, LANES))

    for k in range(CHUNKS):
        cut = slice(k * LANES, (k + 1) * LANES)
        raw[k * RAW : k * RAW + 12, :] = params_ref[:, cut]
        raw[k * RAW + 12 : k * RAW + 15, :] = points_ref[:, cut]
        raw[k * RAW + 16 : k * RAW + 18, :] = frames_ref[:, cut]

    def row(q):
        return raw[pl.ds(q, CHUNKS, stride=RAW), :]

    f = pixel_frame(row, ids_ref[...], camera_ref)
    entries = {
        AX2: f["ax2"], AY2: f["ay2"], IX2: f["ix2"], IY2: f["iy2"],
        VT: f["vt"], VB: f["vb"], VN: f["vn"],
        PT: inner_three(f["point"], f["tangent"]),
        PB: inner_three(f["point"], f["bitangent"]),
        PN: inner_three(f["point"], f["normal"]),
        KG: 4.0 * f["rcv"] / (math.pi * f["ax"] * f["ay"]),
        F0: row(11), F1: 1.0 - row(11), K5: (1.0 - row(11)) * (5.0 * math.sqrt(2.0) / 4.0),
    }
    for c in range(3):
        entries[TX + c], entries[BX + c], entries[NX + c] = f["tangent"][c], f["bitangent"][c], f["normal"][c]
        entries[KD0 + c] = row(c) * (1.0 / math.pi)
        entries[KS0 + c] = row(3 + c)
    for q, value in entries.items():
        table[q] = value

    rows = SUBS * GROUP

    def chunk(k, _):
        cut = pl.ds(pl.multiple_of(k * LANES, LANES), LANES)

        def px(q):
            return jnp.broadcast_to(table[q, pl.ds(k, 1), :], (rows, LANES))

        total = None
        squares = None
        for g in range(lights // rows):
            at = slice(g * rows, (g + 1) * rows)
            visible = shadow_ref[at, cut].astype(jnp.float32)
            measured = [observed_ref[c, at, cut].astype(jnp.float32) for c in range(3)]
            sums, light_terms, square = pair_terms(
                px, [light_wide[q, at, :] for q in range(6)], visible, measured
            )
            sums = [fold(x) for x in sums]
            square = fold(square)
            total = sums if total is None else [a + b for a, b in zip(total, sums)]
            squares = square if squares is None else squares + square
            for q in range(6):
                light_sum[q, at, :] += light_terms[q]
        square_sum[...] += squares
        for q in range(SUMS):
            sums_ref[pl.ds(pl.multiple_of(q * BLOCK // LANES * SUBS + k * SUBS, SUBS), SUBS), :] = total[q]
        return 0

    lax.fori_loop(0, CHUNKS, chunk, 0)

    def summed(q):
        start = q * CHUNKS * SUBS
        parts = [sums_ref[pl.ds(start + i, CHUNKS, stride=SUBS), :] for i in range(SUBS)]
        while len(parts) > 1:
            parts = [a + b for a, b in zip(parts[::2], parts[1::2])]
        return parts[0]

    z = [summed(q) for q in range(SUMS)]
    vt, vb, vn = f["vt"], f["vb"], f["vn"]
    uv = z[SH] * f["rwv"] * f["rcv"]
    wv = -z[SH] * f["rwv"] * f["cv"] * f["vroot"]
    u11, u22, u12 = z[U11] + uv * vt * vt, z[U22] + uv * vb * vb, z[U12] + uv * vt * vb
    u13, u23 = z[U13] + uv * vt * vn, z[U23] + uv * vb * vn
    wt, wb = z[WT] + wv * vt, z[WB] + wv * vb
    ax2, ay2, ix2, iy2 = f["ax2"], f["ay2"], f["ix2"], f["iy2"]
    tau_x = (1.0 - iy2) * z[V23] - ay2 * u23 - wb
    tau_y = (ix2 - 1.0) * z[V13] + ax2 * u13 + wt
    tau_z = (iy2 - ix2) * z[V12] + (ay2 - ax2) * u12
    turned = tau_x + f["inv"] * f["along"] * tau_z
    grads = [z[SD0 + c] * (1.0 / math.pi) for c in range(3)] + [z[SS0 + c] for c in range(3)]
    grads.append(ix2 * z[V11] - ax2 * u11 - z[SH])
    grads.append(iy2 * z[V22] - ay2 * u22 - z[SH])
    grads.append(f["kappa"] * (f["t_loc"][1] * tau_y - f["b_loc"][1] * turned))
    grads.append(f["kappa"] * (f["t_loc"][2] * tau_y - f["b_loc"][2] * turned))
    grads.append(tau_z * f["inv"] * f["inv"] * f["kappa"])
    grads.append(z[SF])
    for q in range(ROWS):
        grads_ref[pl.ds(q, CHUNKS, stride=ROWS), :] = grads[q]

    @pl.when(step == pl.num_programs(0) - 1)
    def _():
        wide = lax.broadcasted_iota(jnp.int32, (SUBS, LANES), 1)
        deep = lax.broadcasted_iota(jnp.int32, (SUBS, LANES), 0)
        lines = []
        for q in range(6):
            spread = jnp.zeros((SUBS, LANES), jnp.float32)
            for g in range(groups):
                line = jnp.sum(light_sum[q, g * SUBS : (g + 1) * SUBS, :], axis=1, keepdims=True)
                spread = jnp.where(wide == deep + g * SUBS, line, spread)
            lines.append(jnp.sum(spread, axis=0, keepdims=True))
        lines.append(jnp.sum(square_sum[...], axis=0, keepdims=True))
        tile = jnp.zeros((SUBS, LANES), jnp.float32)
        for q, line in enumerate(lines):
            tile = jnp.where(deep == q, line, tile)
        light_ref[...] = tile


def local_gradients(observed, shadow, view_ids, points, frames, params, power, pos, cameras):
    lights, pixels = shadow.shape
    steps = pixels // BLOCK
    return pl.pallas_call(
        gradient_kernel,
        grid=(steps,),
        in_specs=[
            pl.BlockSpec(memory_space=pltpu.SMEM),
            pl.BlockSpec((3, lights, BLOCK), lambda i: (0, 0, i)),
            pl.BlockSpec((lights, BLOCK), lambda i: (0, i)),
            pl.BlockSpec((CHUNKS, LANES), lambda i: (i, 0)),
            pl.BlockSpec((3, BLOCK), lambda i: (0, i)),
            pl.BlockSpec((2, BLOCK), lambda i: (0, i)),
            pl.BlockSpec((ROWS, BLOCK), lambda i: (0, i)),
            pl.BlockSpec((3, lights), lambda i: (0, 0)),
            pl.BlockSpec((3, lights), lambda i: (0, 0)),
        ],
        out_specs=[
            pl.BlockSpec((CHUNKS * ROWS, LANES), lambda i: (i, 0)),
            pl.BlockSpec((SUBS, LANES), lambda i: (0, 0)),
        ],
        out_shape=[
            jax.ShapeDtypeStruct((pixels // LANES * ROWS, LANES), jnp.float32),
            jax.ShapeDtypeStruct((SUBS, LANES), jnp.float32),
        ],
        scratch_shapes=[
            pltpu.VMEM((CHUNKS * RAW, LANES), jnp.float32),
            pltpu.VMEM((TABLE, SUBS, LANES), jnp.float32),
            pltpu.VMEM((SUMS * CHUNKS * SUBS, LANES), jnp.float32),
            pltpu.VMEM((6, lights, LANES), jnp.float32),
            pltpu.VMEM((6, lights, LANES), jnp.float32),
            pltpu.VMEM((SUBS, LANES), jnp.float32),
        ],
        name="pair_gradients",
    )(cameras, observed, shadow, view_ids.reshape(pixels // LANES, LANES), points, frames, params, power, pos)


def share_kernel(arrived_ref, lights_ref, out_ref):
    parts, rows = arrived_ref.shape[:2]
    for at in range(0, rows, SUBS):
        total = arrived_ref[0, at : at + SUBS, :]
        for i in range(1, parts):
            total = total + arrived_ref[i, at : at + SUBS, :]
        for i in range(parts):
            out_ref[i, at : at + SUBS, :] = total
    tile = lights_ref[0]
    for i in range(1, lights_ref.shape[0]):
        tile = tile + lights_ref[i]
    for i in range(parts):
        out_ref[i, rows : rows + SUBS, :] = tile


def square_kernel(gathered_ref, out_ref):
    parts, rows = gathered_ref.shape[0], gathered_ref.shape[1] - SUBS
    lines = []
    for at in range(0, rows, SUBS):
        total = jnp.zeros((SUBS, LANES), jnp.float32)
        for i in range(parts):
            value = gathered_ref[i, at : at + SUBS, :]
            total = total + value * value
        lines.append(total)
    total = functools.reduce(jnp.add, lines)
    for i in range(out_ref.shape[0]):
        out_ref[i] = total


def whole(x):
    return jnp.sum(jnp.sum(x, axis=0, keepdims=True), axis=1, keepdims=True)


def step_kernel(
    pixel_total, light_total, gathered_ref, squares_ref, own_ref, params_ref, power_ref, pos_ref,
    new_params_ref, new_power_ref, new_pos_ref, loss_ref,
):
    parts, rows = gathered_ref.shape[0], gathered_ref.shape[1] - SUBS
    total = squares_ref[0]
    for i in range(1, squares_ref.shape[0]):
        total = total + squares_ref[i]
    pixel_scale = STRIDE * lax.rsqrt(whole(total) / (ROWS * pixel_total) + EPS)
    deep = lax.broadcasted_iota(jnp.int32, (SUBS, LANES), 0)
    light_sq = jnp.zeros((SUBS, LANES), jnp.float32)
    residual_sq = jnp.zeros((SUBS, LANES), jnp.float32)
    for i in range(parts):
        tile = gathered_ref[i, rows : rows + SUBS, :]
        light_sq = light_sq + jnp.where(deep < 6, tile * tile, 0.0)
        residual_sq = residual_sq + jnp.where(deep == 6, tile, 0.0)
    light_scale = STRIDE * lax.rsqrt(whole(light_sq) / (6 * light_total) + EPS)
    loss_ref[...] = whole(residual_sq) / (3.0 * light_total * pixel_total)
    lights = power_ref.shape[1]
    new_power_ref[...] = power_ref[...] - own_ref[0:3, :lights] * light_scale
    new_pos_ref[...] = pos_ref[...] - own_ref[3:6, :lights] * light_scale
    chunks = rows // ROWS
    for i in range(parts):
        for k in range(chunks):
            cut = slice((i * chunks + k) * LANES, (i * chunks + k + 1) * LANES)
            grad = gathered_ref[i, k * ROWS : (k + 1) * ROWS, :]
            new_params_ref[:, cut] = params_ref[:, cut] - grad * pixel_scale


def broadcast_exchange(x, axes):
    return lax.all_to_all(x, axes, split_axis=0, concat_axis=0, tiled=True)


def shards(observed, shadow, view_ids, points, frames, params, power, pos, cameras):
    lights, pixels = shadow.shape
    px_size, lt_size = lax.axis_size(PX), lax.axis_size(LT)
    grads, light_tile = local_gradients(
        observed, shadow, view_ids, points, frames, params, power, pos, cameras
    )
    share_rows = grads.shape[0] // lt_size
    arrived = broadcast_exchange(grads.reshape(lt_size, share_rows, LANES), LT)
    light_parts = broadcast_exchange(
        jnp.broadcast_to(light_tile[None], (px_size, SUBS, LANES)), PX
    )
    spread = pl.pallas_call(
        share_kernel,
        out_shape=jax.ShapeDtypeStruct((lt_size, share_rows + SUBS, LANES), jnp.float32),
        name="share_sum",
    )(arrived, light_parts)
    own_lights = spread[0, share_rows:, :]
    gathered = broadcast_exchange(spread, LT)
    squares = pl.pallas_call(
        square_kernel,
        out_shape=jax.ShapeDtypeStruct((px_size, SUBS, LANES), jnp.float32),
        name="block_squares",
    )(gathered)
    squares = broadcast_exchange(squares, PX)
    new_params, new_power, new_pos, loss = pl.pallas_call(
        functools.partial(step_kernel, pixels * px_size, lights * lt_size),
        out_shape=(
            jax.ShapeDtypeStruct(params.shape, jnp.float32),
            jax.ShapeDtypeStruct(power.shape, jnp.float32),
            jax.ShapeDtypeStruct(pos.shape, jnp.float32),
            jax.ShapeDtypeStruct((1, 1), jnp.float32),
        ),
        name="step",
    )(gathered, squares, own_lights, params, power, pos)
    return new_params, new_power, new_pos, loss.reshape(())


def solution(mesh):
    torus = Mesh(mesh.devices.reshape(4, 4, 2, 8, 2), PX + LT)
    placed = (
        P(None, LT, PX),
        P(LT, PX),
        P(PX),
        P(None, PX),
        P(None, PX),
        P(None, PX),
        P(None, LT),
        P(None, LT),
        P(),
    )
    return jax.shard_map(
        shards,
        mesh=torus,
        in_specs=placed,
        out_specs=(P(None, PX), P(None, LT), P(None, LT), P()),
        check_vma=False,
    )
```

time: 273 us -> 105 us (0.38)
  the two profiles are of different devices: /device:TPU:2 before, /device:TPU:1 now
where the time goes in v1:
time: 105 us; the launch traced here: 104 us
  blocking collectives  64.1 us (61%)
  Pallas kernels  19.4 us (18%)
  waiting for transfers between devices  9.46 us (9%)
  starting transfers between devices  8.04 us (8%)
  local copies, waits for them, and re-layouts  2.62 us (2%)
    all_to_all x3, blocking collectives, broadcast_exchange(): return lax.all_to_all(x, axes, split_axis=0, concat_axis=0, tiled=True)  64.1 us
    pallas_call x1, Pallas kernels, local_gradients(): pl.pallas_call(gradient_kernel, grid=(steps,), in_specs=[pl.BlockSpec(mem...  13.6 us
    all_to_all x1, waiting for transfers between devices, broadcast_exchange(): return lax.all_to_all(x, axes, split_axis=0, concat_axis=0, tiled=True)  9.46 us
    all_to_all x1, starting transfers between devices, broadcast_exchange(): return lax.all_to_all(x, axes, split_axis=0, concat_axis=0, tiled=True)  8.04 us
    pallas_call x1, Pallas kernels, shards(): pl.pallas_call(functools.partial(step_kernel, pixels * px_size, lights *...  2.23 us
  transfers between devices with their start and end apart: 1, of which 1 were waited for; matrix products, arithmetic and copies ran while one was open for 1% of the time, Pallas kernels for 0%

profile of v1, /device:TPU:1, one launch (start us, length us, event | category | flops | bytes accessed | tf_op | source)
XLA Modules:
  0.0 104.3 jit_solution(16363654633203319930)
XLA Ops:
  0.6 13.6 %pair_gradients.1 = (f32[768,128]{1,0:T(8,128)}, f32[8,128]{1,0:T(8,128)}) custom-call(f32[3,16]{1,0:T(4,128)} %camera_ref.1, bf16[3,32,8192]{2,1,0:T(8,128)(2,1)} %observed_ref.1, s32[32,8192]{1,0:T(8,128)} %shadow_ref.1, s32[64,128]{1,0:T(8,128)} %bitcast.6, f32[3,8192]{1,0:T(4,128)} %points_ref.1, f32[2,8192]{1,0:T(2,128)} %frames_ref.1, ...), custom_call_target="tpu_custom_call" | custom-call | tf_op jit(solution)/shard_map/pair_gradients/pallas_call | solution.py:297
  14.3 0.7 broadcast_in_dim.2
  15.0 25.6 %all_to_all.20.lights_ref = f32[32,8,128]{2,1,0:T(8,128)} all-to-all(f32[32,8,128]{2,1,0:T(8,128)S(1)} %broadcast_in_dim.2), channel_id=1, replica_groups=mesh['px_0'=4,'px_1'=4,'px_2'=2,'lt_0'=8,'lt_1'=2] {'px_0','px_1','px_2'}, dimensions={0} | all-to-all | bytes 262144 | tf_op jit(solution)/shard_map/all_to_all | solution.py:394
  40.6 21.2 %all_to_all.21.arrived_ref = f32[16,48,128]{2,1,0:T(8,128)} all-to-all(f32[16,48,128]{2,1,0:T(8,128)} %bitcast.5), channel_id=1, replica_groups=mesh['px_0'=4,'px_1'=4,'px_2'=2,'lt_0'=8,'lt_1'=2] {'lt_0','lt_1'}, dimensions={0} | all-to-all | bytes 786432 | tf_op jit(solution)/shard_map/all_to_all | solution.py:394
  61.8 1.8 %share_sum.1 = f32[16,56,128]{2,1,0:T(8,128)} custom-call(f32[16,48,128]{2,1,0:T(8,128)} %all_to_all.21.arrived_ref, f32[32,8,128]{2,1,0:T(8,128)} %all_to_all.20.lights_ref), custom_call_target="tpu_custom_call" | custom-call | tf_op jit(solution)/shard_map/share_sum/pallas_call | solution.py:408
  63.7 17.2 %all_to_all.22.gathered_ref = f32[16,56,128]{2,1,0:T(8,128)} all-to-all(f32[16,56,128]{2,1,0:T(8,128)} %share_sum.1), channel_id=1, replica_groups=mesh['px_0'=4,'px_1'=4,'px_2'=2,'lt_0'=8,'lt_1'=2] {'lt_0','lt_1'}, dimensions={0} | all-to-all | bytes 917504 | tf_op jit(solution)/shard_map/all_to_all | solution.py:394
  80.9 1.7 %block_squares.1 = f32[32,8,128]{2,1,0:T(8,128)} custom-call(f32[16,56,128]{2,1,0:T(8,128)} %all_to_all.22.gathered_ref), custom_call_target="tpu_custom_call" | custom-call | tf_op jit(solution)/shard_map/block_squares/pallas_call | solution.py:415
  82.6 8.0 %all-to-all-start.3 = ((f32[32,8,128]{2,1,0:T(8,128)}), f32[32,8,128]{2,1,0:T(8,128)S(1)}, u32[]{:S(2)}, u32[]{:S(2)}) async-start(f32[32,8,128]{2,1,0:T(8,128)} %block_squares.1), calls=%async_computation.3 | async-start | bytes 262144 | tf_op jit(solution)/shard_map/all_to_all | solution.py:394
  90.6 1.3 %slice_bitcast_fusion.own_ref = f32[8,128]{1,0:T(8,128)} fusion(f32[16,56,128]{2,1,0:T(8,128)} %share_sum.1), kind=kLoop, calls=%fused_computation | loop fusion | bytes 8192 | tf_op jit(solution)/shard_map/squeeze | solution.py:413
  91.9 9.5 %all-to-all-done.3.squares_ref = f32[32,8,128]{2,1,0:T(8,128)S(1)} async-done(((f32[32,8,128]{2,1,0:T(8,128)}), f32[32,8,128]{2,1,0:T(8,128)S(1)}, u32[]{:S(2)}, u32[]{:S(2)}) %all-to-all-start.3) | async-done | bytes 131104 | tf_op jit(solution)/shard_map/all_to_all | solution.py:394
  101.4 0.0 copy-start
  101.4 0.7 copy-done
  102.0 2.2 %step.1 = (f32[12,8192]{1,0:T(8,128)}, f32[3,32]{1,0:T(4,128)}, f32[3,32]{1,0:T(4,128)}, f32[1,1]{1,0:T(1,128)}) custom-call(f32[16,56,128]{2,1,0:T(8,128)} %all_to_all.22.gathered_ref, f32[32,8,128]{2,1,0:T(8,128)} %copy-done, f32[8,128]{1,0:T(8,128)} %slice_bitcast_fusion.own_ref, f32[12,8192]{1,0:T(8,128)} %params_ref.3, f32[3,32]{1,0:T(4,128)} %power_ref.3, ...), custom_call_target="tpu_custom_call" | custom-call | tf_op jit(solution)/shard_map/step/pallas_call | solution.py:421
Async XLA Ops:
  82.6 18.8 %all-to-all-start.3 = ((f32[32,8,128]{2,1,0:T(8,128)}), f32[32,8,128]{2,1,0:T(8,128)S(1)}, u32[]{:S(2)}, u32[]{:S(2)}) async-start(f32[32,8,128]{2,1,0:T(8,128)} %block_squares.1), calls=%async_computation.3 | async-start | bytes 262144 | tf_op jit(solution)/shard_map/all_to_all | solution.py:394
  101.4 0.7 copy-start

commit v2 on v1

--- a/solution.py
+++ b/solution.py
@@ -158,6 +158,10 @@
     return sums, light_terms, squares
 
 
+def whole(x):
+    return jnp.sum(jnp.sum(x, axis=0, keepdims=True), axis=1, keepdims=True)
+
+
 def fold(x):
     total = x[:SUBS]
     for g in range(1, x.shape[0] // SUBS):
@@ -278,17 +282,16 @@
         wide = lax.broadcasted_iota(jnp.int32, (SUBS, LANES), 1)
         deep = lax.broadcasted_iota(jnp.int32, (SUBS, LANES), 0)
         lines = []
-        for q in range(6):
+        for kind in range(2):
             spread = jnp.zeros((SUBS, LANES), jnp.float32)
-            for g in range(groups):
-                line = jnp.sum(light_sum[q, g * SUBS : (g + 1) * SUBS, :], axis=1, keepdims=True)
-                spread = jnp.where(wide == deep + g * SUBS, line, spread)
+            for q in range(3):
+                for g in range(groups):
+                    line = jnp.sum(light_sum[3 * kind + q, g * SUBS : (g + 1) * SUBS, :], axis=1, keepdims=True)
+                    spread = jnp.where(wide == deep + (g * SUBS + q * lights), line, spread)
             lines.append(jnp.sum(spread, axis=0, keepdims=True))
-        lines.append(jnp.sum(square_sum[...], axis=0, keepdims=True))
-        tile = jnp.zeros((SUBS, LANES), jnp.float32)
-        for q, line in enumerate(lines):
-            tile = jnp.where(deep == q, line, tile)
-        light_ref[...] = tile
+        first = lax.broadcasted_iota(jnp.int32, (1, LANES), 1)
+        light_ref[0:1, :] = jnp.where(first == 3 * lights, whole(square_sum[...]), lines[0])
+        light_ref[1:2, :] = lines[1]
 
 
 def local_gradients(observed, shadow, view_ids, points, frames, params, power, pos, cameras):
@@ -310,11 +313,11 @@
         ],
         out_specs=[
             pl.BlockSpec((CHUNKS * ROWS, LANES), lambda i: (i, 0)),
-            pl.BlockSpec((SUBS, LANES), lambda i: (0, 0)),
+            pl.BlockSpec((2, LANES), lambda i: (0, 0)),
         ],
         out_shape=[
             jax.ShapeDtypeStruct((pixels // LANES * ROWS, LANES), jnp.float32),
-            jax.ShapeDtypeStruct((SUBS, LANES), jnp.float32),
+            jax.ShapeDtypeStruct((2, LANES), jnp.float32),
         ],
         scratch_shapes=[
             pltpu.VMEM((CHUNKS * RAW, LANES), jnp.float32),
@@ -324,64 +327,73 @@
             pltpu.VMEM((6, lights, LANES), jnp.float32),
             pltpu.VMEM((SUBS, LANES), jnp.float32),
         ],
+        compiler_params=pltpu.CompilerParams(vmem_limit_bytes=16 << 20),
         name="pair_gradients",
-    )(cameras, observed, shadow, view_ids.reshape(pixels // LANES, LANES), points, frames, params, power, pos)
-
-
-def share_kernel(arrived_ref, lights_ref, out_ref):
+    )(
+        *(
+            pltpu.with_memory_space_constraint(x, pltpu.HBM)
+            for x in (
+                cameras, observed, shadow, view_ids.reshape(pixels // LANES, LANES),
+                points, frames, params, power, pos,
+            )
+        )
+    )
+
+
+def share_kernel(mark, arrived_ref, light_ref, share_ref, spread_ref):
     parts, rows = arrived_ref.shape[:2]
+    squares = jnp.zeros((SUBS, LANES), jnp.float32)
     for at in range(0, rows, SUBS):
-        total = arrived_ref[0, at : at + SUBS, :]
-        for i in range(1, parts):
-            total = total + arrived_ref[i, at : at + SUBS, :]
-        for i in range(parts):
-            out_ref[i, at : at + SUBS, :] = total
-    tile = lights_ref[0]
-    for i in range(1, lights_ref.shape[0]):
-        tile = tile + lights_ref[i]
-    for i in range(parts):
-        out_ref[i, rows : rows + SUBS, :] = tile
-
-
-def square_kernel(gathered_ref, out_ref):
-    parts, rows = gathered_ref.shape[0], gathered_ref.shape[1] - SUBS
-    lines = []
+        pieces = [arrived_ref[i, at : at + SUBS, :] for i in range(parts)]
+        while len(pieces) > 1:
+            pieces = [a + b for a, b in zip(pieces[::2], pieces[1::2])]
+        share_ref[at : at + SUBS, :] = pieces[0]
+        squares = squares + pieces[0] * pieces[0]
+    lane = lax.broadcasted_iota(jnp.int32, (2, LANES), 1)
+    deep = lax.broadcasted_iota(jnp.int32, (2, LANES), 0)
+    tile = jnp.where((lane == mark) & (deep == 1), whole(squares), light_ref[...])
+    for i in range(spread_ref.shape[0]):
+        spread_ref[i] = tile
+
+
+def join_kernel(mark, share_ref, light_parts_ref, out_ref, light_ref):
+    tile = light_parts_ref[0]
+    for i in range(1, light_parts_ref.shape[0]):
+        tile = tile + light_parts_ref[i]
+    light_ref[...] = tile
+    lane = lax.broadcasted_iota(jnp.int32, (2, LANES), 1)
+    light_sq = whole(jnp.where(lane < mark, tile * tile, 0.0))
+    deep = lax.broadcasted_iota(jnp.int32, (SUBS, LANES), 0)
+    wide = lax.broadcasted_iota(jnp.int32, (SUBS, LANES), 1)
+    tail = jnp.where(wide == 0, light_sq, 0.0)
+    tail = jnp.where(wide == 1, tile[0:1, mark : mark + 1], tail)
+    tail = jnp.where(wide == 2, tile[1:2, mark : mark + 1], tail)
+    tail = jnp.where(deep == 0, tail, 0.0)
+    rows = share_ref.shape[0]
     for at in range(0, rows, SUBS):
-        total = jnp.zeros((SUBS, LANES), jnp.float32)
-        for i in range(parts):
-            value = gathered_ref[i, at : at + SUBS, :]
-            total = total + value * value
-        lines.append(total)
-    total = functools.reduce(jnp.add, lines)
+        value = share_ref[at : at + SUBS, :]
+        for i in range(out_ref.shape[0]):
+            out_ref[i, at : at + SUBS, :] = value
     for i in range(out_ref.shape[0]):
-        out_ref[i] = total
-
-
-def whole(x):
-    return jnp.sum(jnp.sum(x, axis=0, keepdims=True), axis=1, keepdims=True)
+        out_ref[i, rows : rows + SUBS, :] = tail
 
 
 def step_kernel(
-    pixel_total, light_total, gathered_ref, squares_ref, own_ref, params_ref, power_ref, pos_ref,
+    pixel_total, light_total, gathered_ref, light_ref, params_ref, power_ref, pos_ref,
     new_params_ref, new_power_ref, new_pos_ref, loss_ref,
 ):
     parts, rows = gathered_ref.shape[0], gathered_ref.shape[1] - SUBS
-    total = squares_ref[0]
-    for i in range(1, squares_ref.shape[0]):
-        total = total + squares_ref[i]
-    pixel_scale = STRIDE * lax.rsqrt(whole(total) / (ROWS * pixel_total) + EPS)
-    deep = lax.broadcasted_iota(jnp.int32, (SUBS, LANES), 0)
-    light_sq = jnp.zeros((SUBS, LANES), jnp.float32)
-    residual_sq = jnp.zeros((SUBS, LANES), jnp.float32)
-    for i in range(parts):
-        tile = gathered_ref[i, rows : rows + SUBS, :]
-        light_sq = light_sq + jnp.where(deep < 6, tile * tile, 0.0)
-        residual_sq = residual_sq + jnp.where(deep == 6, tile, 0.0)
-    light_scale = STRIDE * lax.rsqrt(whole(light_sq) / (6 * light_total) + EPS)
-    loss_ref[...] = whole(residual_sq) / (3.0 * light_total * pixel_total)
+    tail = gathered_ref[0, rows : rows + SUBS, :]
+    for i in range(1, parts):
+        tail = tail + gathered_ref[i, rows : rows + SUBS, :]
+    light_scale = STRIDE * lax.rsqrt(tail[0:1, 0:1] / (6 * light_total) + EPS)
+    pixel_scale = STRIDE * lax.rsqrt(tail[0:1, 2:3] / (ROWS * pixel_total) + EPS)
+    loss_ref[...] = tail[0:1, 1:2] / (3.0 * light_total * pixel_total)
     lights = power_ref.shape[1]
-    new_power_ref[...] = power_ref[...] - own_ref[0:3, :lights] * light_scale
-    new_pos_ref[...] = pos_ref[...] - own_ref[3:6, :lights] * light_scale
+    for c in range(3):
+        cut = slice(c * lights, (c + 1) * lights)
+        new_power_ref[c : c + 1, :] = power_ref[c : c + 1, :] - light_ref[0:1, cut] * light_scale
+        new_pos_ref[c : c + 1, :] = pos_ref[c : c + 1, :] - light_ref[1:2, cut] * light_scale
     chunks = rows // ROWS
     for i in range(parts):
         for k in range(chunks):
@@ -401,23 +413,29 @@
         observed, shadow, view_ids, points, frames, params, power, pos, cameras
     )
     share_rows = grads.shape[0] // lt_size
+    mark = 3 * lights
+    small = pltpu.CompilerParams(vmem_limit_bytes=8 << 20)
     arrived = broadcast_exchange(grads.reshape(lt_size, share_rows, LANES), LT)
-    light_parts = broadcast_exchange(
-        jnp.broadcast_to(light_tile[None], (px_size, SUBS, LANES)), PX
-    )
-    spread = pl.pallas_call(
-        share_kernel,
-        out_shape=jax.ShapeDtypeStruct((lt_size, share_rows + SUBS, LANES), jnp.float32),
+    share, spread = pl.pallas_call(
+        functools.partial(share_kernel, mark),
+        out_shape=(
+            jax.ShapeDtypeStruct((share_rows, LANES), jnp.float32),
+            jax.ShapeDtypeStruct((px_size, 2, LANES), jnp.float32),
+        ),
+        compiler_params=small,
         name="share_sum",
-    )(arrived, light_parts)
-    own_lights = spread[0, share_rows:, :]
-    gathered = broadcast_exchange(spread, LT)
-    squares = pl.pallas_call(
-        square_kernel,
-        out_shape=jax.ShapeDtypeStruct((px_size, SUBS, LANES), jnp.float32),
-        name="block_squares",
-    )(gathered)
-    squares = broadcast_exchange(squares, PX)
+    )(arrived, light_tile)
+    light_parts = broadcast_exchange(spread, PX)
+    joined, own_lights = pl.pallas_call(
+        functools.partial(join_kernel, mark),
+        out_shape=(
+            jax.ShapeDtypeStruct((lt_size, share_rows + SUBS, LANES), jnp.float32),
+            jax.ShapeDtypeStruct((2, LANES), jnp.float32),
+        ),
+        compiler_params=small,
+        name="join",
+    )(share, light_parts)
+    gathered = broadcast_exchange(joined, LT)
     new_params, new_power, new_pos, loss = pl.pallas_call(
         functools.partial(step_kernel, pixels * px_size, lights * lt_size),
         out_shape=(
@@ -426,8 +444,9 @@
             jax.ShapeDtypeStruct(pos.shape, jnp.float32),
             jax.ShapeDtypeStruct((1, 1), jnp.float32),
         ),
+        compiler_params=small,
         name="step",
-    )(gathered, squares, own_lights, params, power, pos)
+    )(gathered, own_lights, params, power, pos)
     return new_params, new_power, new_pos, loss.reshape(())
 
 

time: 105 us -> 79.2 us (0.75)
  waiting for transfers between devices: 9.46 us -> 0 us
  starting transfers between devices: 8.04 us -> 0 us
  Pallas kernels: 19.4 us -> 14.2 us
  local copies, waits for them, and re-layouts: 2.62 us -> 0.02 us
    all_to_all x1 -> x0, waiting for transfers between devices: 9.46 us -> none  [broadcast_exchange(): return lax.all_to_all(x, axes, split_axis=0, concat_axis=0, tiled=True)]
    all_to_all x1 -> x0, starting transfers between devices: 8.04 us -> none  [broadcast_exchange(): return lax.all_to_all(x, axes, split_axis=0, concat_axis=0, tiled=True)]
    pallas_call x2, Pallas kernels: 3.55 us -> 0.26 us  [the longest x1 0.14 us: shards(): pl.pallas_call(functools.partial(join_kernel, mark), out_shape=(jax.Shape...]
    squeeze x1 -> x0, local copies, waits for them, and re-layouts: 1.28 us -> none  [shards(): own_lights = spread[0, share_rows:, :]]
    pallas_call x1, Pallas kernels: 2.23 us -> 0.98 us  [shards(): pl.pallas_call(functools.partial(step_kernel, pixels * px_size, lights *...]
  transfers between devices with their start and end apart: 1 -> 0, of which waited for: 1 -> 0; matrix products, arithmetic and copies ran while one was open for 1% -> 0% of each run, Pallas kernels for 0% -> 0%
where the time goes in v2:
time: 79.2 us; the launch traced here: 78.5 us
  blocking collectives  63.6 us (80%)
  Pallas kernels  14.2 us (18%)
    all_to_all x3, blocking collectives, broadcast_exchange(): return lax.all_to_all(x, axes, split_axis=0, concat_axis=0, tiled=True)  63.6 us
    pallas_call x1, Pallas kernels, local_gradients(): pl.pallas_call(gradient_kernel, grid=(steps,), in_specs=[pl.BlockSpec(mem...  13 us

profile of v2, /device:TPU:1, one launch (start us, length us, event | category | flops | bytes accessed | tf_op | source)
XLA Modules:
  0.0 78.5 jit_solution(3801865152693995229)
XLA Ops:
  0.6 13.0 %pair_gradients.1 = (f32[768,128]{1,0:T(8,128)S(1)}, f32[2,128]{1,0:T(2,128)S(1)}) custom-call(f32[3,16]{1,0:T(4,128)} %camera_ref.1, bf16[3,32,8192]{2,1,0:T(8,128)(2,1)} %observed_ref.1, s32[32,8192]{1,0:T(8,128)} %shadow_ref.1, s32[64,128]{1,0:T(8,128)} %bitcast.4, f32[3,8192]{1,0:T(4,128)} %points_ref.1, f32[2,8192]{1,0:T(2,128)} %frames_ref.1, ...), custom_call_target="tpu_custom_call" | custom-call | tf_op jit(solution)/shard_map/pair_gradients/pallas_call | solution.py:300
  13.6 0.0 copy-start
  13.6 0.0 copy-start.1
  13.6 0.0 copy-start.2
  13.6 22.9 %all_to_all.15.arrived_ref = f32[16,48,128]{2,1,0:T(8,128)S(1)} all-to-all(f32[16,48,128]{2,1,0:T(8,128)S(1)} %bitcast.3), channel_id=1, replica_groups=mesh['px_0'=4,'px_1'=4,'px_2'=2,'lt_0'=8,'lt_1'=2] {'lt_0','lt_1'}, dimensions={0} | all-to-all | bytes 786432 | tf_op jit(solution)/shard_map/all_to_all | solution.py:406
  36.5 0.1 share_sum.1
  36.6 23.5 %all_to_all.16.light_parts_ref = f32[32,2,128]{2,1,0:T(2,128)S(1)} all-to-all(f32[32,2,128]{2,1,0:T(2,128)S(1)} %get-tuple-element.17), channel_id=1, replica_groups=mesh['px_0'=4,'px_1'=4,'px_2'=2,'lt_0'=8,'lt_1'=2] {'px_0','px_1','px_2'}, dimensions={0} | all-to-all | bytes 65536 | tf_op jit(solution)/shard_map/all_to_all | solution.py:406
  60.1 0.1 join.1
  60.3 17.3 %all_to_all.17.gathered_ref = f32[16,56,128]{2,1,0:T(8,128)S(1)} all-to-all(f32[16,56,128]{2,1,0:T(8,128)S(1)} %get-tuple-element.18), channel_id=1, replica_groups=mesh['px_0'=4,'px_1'=4,'px_2'=2,'lt_0'=8,'lt_1'=2] {'lt_0','lt_1'}, dimensions={0} | all-to-all | bytes 917504 | tf_op jit(solution)/shard_map/all_to_all | solution.py:406
  77.5 0.0 copy-done
  77.5 0.0 copy-done.1
  77.5 0.0 copy-done.2
  77.5 1.0 %step.1 = (f32[12,8192]{1,0:T(8,128)}, f32[3,32]{1,0:T(4,128)}, f32[3,32]{1,0:T(4,128)}, f32[1,1]{1,0:T(1,128)}) custom-call(f32[16,56,128]{2,1,0:T(8,128)S(1)} %all_to_all.17.gathered_ref, f32[2,128]{1,0:T(2,128)S(1)} %get-tuple-element.19.light_ref, f32[12,8192]{1,0:T(8,128)S(1)} %copy-done, f32[3,32]{1,0:T(4,128)S(1)} %copy-done.1, f32[3,32]{1,0:T(4,128)S(1)} %copy-done.2), custom_call_target="tpu_custom_call" | custom-call | tf_op jit(solution)/shard_map/step/pallas_call | solution.py:439
Async XLA Ops:
  13.6 63.9 %copy-start = (f32[12,8192]{1,0:T(8,128)S(1)}, f32[12,8192]{1,0:T(8,128)}, u32[]{:S(2)}) copy-start(f32[12,8192]{1,0:T(8,128)} %params_ref.3) | copy-start | bytes 1179652
  13.6 63.9 %copy-start.1 = (f32[3,32]{1,0:T(4,128)S(1)}, f32[3,32]{1,0:T(4,128)}, u32[]{:S(2)}) copy-start(f32[3,32]{1,0:T(4,128)} %power_ref.3) | copy-start | bytes 1156
  13.6 63.9 %copy-start.2 = (f32[3,32]{1,0:T(4,128)S(1)}, f32[3,32]{1,0:T(4,128)}, u32[]{:S(2)}) copy-start(f32[3,32]{1,0:T(4,128)} %pos_ref.3) | copy-start | bytes 1156

commit v3 on v2

v3 whole, which is shorter than its diff:
```python
import functools
import math

import jax
import jax.numpy as jnp
from jax import lax
from jax.experimental import pallas as pl
from jax.experimental.pallas import tpu as pltpu
from jax.sharding import Mesh
from jax.sharding import PartitionSpec as P

PX = ("px_0", "px_1", "px_2")
LT = ("lt_0", "lt_1")

SOFT = 0.01
EPS = 1e-06
STRIDE = 0.2
LANES = 128
SUBS = 8
ROWS = 12
BLOCK = 2048
CHUNKS = BLOCK // LANES
RAW = 25
DEPTH = 32
PITCH = 33
SUM_PITCH = 9
UNROLL = 8

(VT, VB, VN, AX2, AY2, IX2, IY2, F0, F1, K5, KD0, KD1, KD2, KS0, KS1, KS2) = range(16)
TABLE = 16
(SD0, SD1, SD2, SS0, SS1, SS2, SF, SH, V11, V22, V12, V13, V23, U11, U22, U12, TX, TY) = range(18)
SUMS = 18
LEFT = (0, 0, 1, 1, 0, 2)
RIGHT = (0, 1, 0, 1, 2, 0)
COMPS = 5
BLOCKS = 5
SQUARED = 3


def inner_three(first, second):
    return first[0] * second[0] + first[1] * second[1] + first[2] * second[2]


def pixel_frame(row, ids, camera_ref):
    azimuth = 2.0 * math.pi * row(17)
    ca, sa = jnp.cos(row(16)), jnp.sin(row(16))
    cz, sz = jnp.cos(azimuth), jnp.sin(azimuth)
    base_n = [sa * cz, sa * sz, ca]
    base_t = [ca * cz, ca * sz, -sa]
    base_b = [-sz, cz]
    u, v, spin = row(8), row(9), row(10)
    cs, sn = jnp.cos(spin), jnp.sin(spin)
    kappa = lax.rsqrt(1.0 + u * u + v * v)
    along = kappa * (u * cs + v * sn)
    inv = lax.rsqrt(1.0 - along * along)
    n_loc = [kappa, kappa * u, kappa * v]
    t_loc = [-along * n_loc[0] * inv, (cs - along * n_loc[1]) * inv, (sn - along * n_loc[2]) * inv]
    kb = kappa * inv
    b_loc = [kb * (u * sn - v * cs), -kb * sn, kb * cs]

    def world(loc):
        return [
            loc[0] * base_n[0] + loc[1] * base_t[0] + loc[2] * base_b[0],
            loc[0] * base_n[1] + loc[1] * base_t[1] + loc[2] * base_b[1],
            loc[0] * base_n[2] + loc[1] * base_t[2],
        ]

    tangent, bitangent, normal = world(t_loc), world(b_loc), world(n_loc)
    point = [row(12), row(13), row(14)]
    camera = [jnp.full_like(u, camera_ref[c, 0]) for c in range(3)]
    for view in range(1, camera_ref.shape[1]):
        chosen = ids == view
        camera = [jnp.where(chosen, camera_ref[c, view], camera[c]) for c in range(3)]
    toward = [camera[c] - point[c] for c in range(3)]
    scale = lax.rsqrt(inner_three(toward, toward))
    view_dir = [toward[c] * scale for c in range(3)]
    vt, vb, vn = (inner_three(view_dir, f) for f in (tangent, bitangent, normal))
    ax, ay = jnp.exp(row(6)), jnp.exp(row(7))
    ax2, ay2 = ax * ax, ay * ay
    ix2, iy2 = 1.0 / ax2, 1.0 / ay2
    vroot = lax.rsqrt(vn * vn + SOFT)
    cv = 0.5 * (vn + (vn * vn + SOFT) * vroot)
    wv2 = cv * cv + ax2 * vt * vt + ay2 * vb * vb
    rwv = lax.rsqrt(wv2)
    rcv = 1.0 / (cv + wv2 * rwv)
    return dict(
        tangent=tangent, bitangent=bitangent, normal=normal, point=point, view_dir=view_dir,
        vt=vt, vb=vb, vn=vn, ax=ax, ay=ay, ax2=ax2, ay2=ay2, ix2=ix2, iy2=iy2,
        inv_f1=1.0 / (1.0 - row(11)), lobe=16.0 * rcv / (math.pi * ax * ay), vroot=vroot, cv=cv, rwv=rwv, rcv=rcv, kappa=kappa, inv=inv, along=along,
        t_loc=t_loc, b_loc=b_loc,
    )


def pair_terms(px, offsets, pw, visible, measured):
    ot, ob, on, d2, ov = offsets
    r = lax.rsqrt(d2)
    id2 = r * r
    lt, lb, ln, lv = ot * r, ob * r, on * r, ov * r
    m = 0.5 * lv + 0.5
    a1, a2, a3 = lt + px(VT), lb + px(VB), ln + px(VN)
    b1, b2 = a1 * px(IX2), a2 * px(IY2)
    rq = lax.rsqrt(b1 * a1 + b2 * a2 + a3 * a3)
    rq = rq * rq
    rm = lax.rsqrt(m)
    om = 1.0 - m * rm
    om2 = om * om
    om4 = om2 * om2
    s5 = om4 * om
    fresnel = px(F0) + px(F1) * s5
    rf = lax.rsqrt(fresnel)
    lsq = ln * ln + SOFT
    rs = lax.rsqrt(lsq)
    cn = ln + lsq * rs
    xt, xb = lt * px(AX2), lb * px(AY2)
    wsq = cn * cn + (xt * lt + xb * lb)
    rw = lax.rsqrt(wsq)
    rc = lax.rsqrt(cn + wsq * rw)
    rc = rc * rc
    cni = cn * (id2 * visible)
    mq = m * rq
    gi = (mq * mq) * (rc * cni) * fresnel
    sums = [None] * SUMS
    power_terms = []
    squares = h = s = None
    for c in range(3):
        diffuse, glossy = pw[c] * cni, pw[c] * gi
        res = px(KD0 + c) * diffuse + px(KS0 + c) * glossy - measured[c]
        squares = res * res if c == 0 else squares + res * res
        sums[SD0 + c], sums[SS0 + c] = res * diffuse, res * glossy
        part = px(KS0 + c) * sums[SS0 + c]
        term = px(KD0 + c) * sums[SD0 + c] + part
        power_terms.append(term)
        h = part if c == 0 else h + part
        s = term if c == 0 else s + term
    squares = squares * visible
    x = (h * rf) * rf
    nm = rm * ((x * om4) * px(K5) - h * rm)
    hw = h * rw
    uu = hw * rc
    ww = rs * (s - hw * cn)
    v4 = (4.0 * h) * rq
    p1, p2 = uu * xt, uu * xb
    q1, q2, q3 = v4 * b1, v4 * b2, v4 * a3
    sums[SF] = x
    sums[SH] = h
    sums[V11], sums[V22], sums[V12] = q1 * a1, q2 * a2, q1 * a2
    sums[V13], sums[V23] = q1 * a3, q2 * a3
    sums[U11], sums[U22], sums[U12] = p1 * lt, p2 * lb, p1 * lb
    sums[TX], sums[TY] = p2 * ln + ww * lb, p1 * ln + ww * lt
    g1, g2, g3 = p1 + q1, p2 + q2, q3 - ww
    inner = (lt * g1 + lb * g2) + (ln * g3 + lv * nm)
    cots = [r * g1, r * g2, r * g3, id2 * (s - 0.5 * inner), r * nm]
    return sums, power_terms, squares, cots


def whole(x):
    return jnp.sum(jnp.sum(x, axis=0, keepdims=True), axis=1, keepdims=True)


def rounded(x):
    return x.astype(jnp.bfloat16).astype(jnp.float32)


def split_three(x):
    first = rounded(x)
    second = rounded(x - first)
    return [first, second, x - first - second]


def gradient_kernel(
    camera_ref, observed_hbm, shadow_hbm, ids_hbm, points_hbm, frames_hbm, params_hbm, power_ref, pos_ref,
    grads_ref, light_ref,
    observed_ref, shadow_ref, ids_ref, points_ref, frames_ref, params_ref,
    raw, table, sums_ref, left, right, offsets, spread_ref, frame_ref, power_wide, power_sum, pos_sum,
    square_sum, sems,
):
    lights, pixels = shadow_hbm.shape
    groups = lights // SUBS
    steps = pixels // BLOCK

    def copies(first, count):
        cut = slice(first * BLOCK, (first + count) * BLOCK)
        tile = slice(first * CHUNKS, (first + count) * CHUNKS)
        slot = min(first, 1)
        pairs = [
            (params_hbm.at[:, cut], params_ref.at[:, cut]),
            (points_hbm.at[:, cut], points_ref.at[:, cut]),
            (frames_hbm.at[:, cut], frames_ref.at[:, cut]),
            (ids_hbm.at[tile, :], ids_ref.at[tile, :]),
            (shadow_hbm.at[:, cut], shadow_ref.at[:, cut]),
            (observed_hbm.at[:, :, cut], observed_ref.at[:, :, cut]),
        ]
        return [pltpu.make_async_copy(a, b, sems.at[slot, i]) for i, (a, b) in enumerate(pairs)]

    stages = [copies(0, 1), copies(1, steps - 1)]
    for copy in stages[0]:
        copy.start()

    power_sum[...] = jnp.zeros_like(power_sum)
    pos_sum[...] = jnp.zeros_like(pos_sum)
    square_sum[...] = jnp.zeros_like(square_sum)
    spread_ref[...] = jnp.zeros_like(spread_ref)
    frame_ref[...] = jnp.zeros_like(frame_ref)
    right[...] = jnp.zeros_like(right)

    def piece(b):
        return slice(b * LANES, (b + 1) * LANES)

    def right_rows(b, q):
        return pl.ds(b * CHUNKS * PITCH + q, CHUNKS, stride=PITCH)

    for i, part in enumerate(RIGHT):
        if part == 0:
            right[right_rows(SQUARED, i * COMPS + 4), :] = jnp.ones((CHUNKS, LANES), jnp.float32)
    lane = lax.broadcasted_iota(jnp.int32, (SUBS, lights), 1)
    sub = lax.broadcasted_iota(jnp.int32, (SUBS, lights), 0)

    def column(source, c, g):
        picked = jnp.where(lane == sub + g * SUBS, source[c : c + 1, :], 0.0)
        return jnp.sum(picked, axis=1, keepdims=True)

    deep_lane = lax.broadcasted_iota(jnp.int32, (SUBS, DEPTH), 1)
    one = jnp.ones((SUBS, DEPTH), jnp.float32)
    zero = jnp.zeros((SUBS, DEPTH), jnp.float32)
    tiles = []
    for g in range(groups):
        at = slice(g * SUBS, (g + 1) * SUBS)
        for c in range(3):
            power_wide[c, at, :] = jnp.broadcast_to(column(power_ref, c, g), (SUBS, LANES))
        pos = [jnp.broadcast_to(column(pos_ref, c, g), (SUBS, DEPTH)) for c in range(3)]
        splits = [split_three(x) for x in pos] + [[one, zero, zero], split_three(inner_three(pos, pos))]
        tile = zero
        for i, part in enumerate(LEFT):
            for c in range(COMPS):
                tile = jnp.where(deep_lane == i * COMPS + c, splits[c][part], tile)
        tiles.append(tile)
    left[...] = jnp.concatenate(tiles, axis=0).astype(jnp.bfloat16)

    def frame(k, depth):
        return jnp.concatenate(
            [right[pl.ds((b * CHUNKS + k) * PITCH, depth), :] for b in range(BLOCKS)], axis=1
        ).astype(jnp.bfloat16)

    def product(k):
        return jnp.dot(left[...], frame(k, DEPTH), preferred_element_type=jnp.float32)

    def gather_positions():
        pos_sum[...] += lax.dot_general(
            spread_ref[...].astype(jnp.bfloat16), frame_ref[...], (((1,), (1,)), ((), ())),
            preferred_element_type=jnp.float32,
        )

    for copy in stages[0][:4]:
        copy.wait()
    for stage in stages[1:]:
        for copy in stage:
            copy.start()

    def arrive(step, first, some):
        for i, stage in enumerate(stages[first:], first):

            @pl.when(step == i)
            def _(stage=stage):
                for copy in stage[some]:
                    copy.wait()

    def block(step, _):
        arrive(step, 1, slice(0, 4))

        base = pl.multiple_of(step * BLOCK, BLOCK)
        for k in range(CHUNKS):
            cut = pl.ds(pl.multiple_of(base + k * LANES, LANES), LANES)
            raw[k * RAW : k * RAW + 12, :] = params_ref[:, cut]
            raw[k * RAW + 12 : k * RAW + 15, :] = points_ref[:, cut]
            raw[k * RAW + 16 : k * RAW + 18, :] = frames_ref[:, cut]

        def row(q):
            return raw[pl.ds(q, CHUNKS, stride=RAW), :]

        ids = ids_ref[pl.ds(pl.multiple_of(step * CHUNKS, CHUNKS), CHUNKS), :]
        f = pixel_frame(row, ids, camera_ref)
        point = f["point"]
        columns = [
            [*vec, -inner_three(point, vec)] for vec in (f["tangent"], f["bitangent"], f["normal"])
        ]
        columns.append([-2.0 * point[c] for c in range(3)] + [inner_three(point, point)])
        columns.append([*f["view_dir"], -inner_three(point, f["view_dir"])])
        for b, column_of in enumerate(columns):
            for c, value in enumerate(column_of):
                rest = value - rounded(value)
                parts = [value, rest, rest - rounded(rest)]
                for i, part in enumerate(RIGHT):
                    right[right_rows(b, i * COMPS + c), :] = parts[part]
        entries = {
            AX2: 4.0 * f["ax2"], AY2: 4.0 * f["ay2"], IX2: f["ix2"], IY2: f["iy2"],
            VT: f["vt"], VB: f["vb"], VN: f["vn"],
            F0: row(11), F1: 1.0 - row(11), K5: 1.25 - 1.25 * row(11),
        }
        for c in range(3):
            entries[KD0 + c] = row(c) * (0.5 / math.pi)
            entries[KS0 + c] = row(3 + c) * f["lobe"]
        for q, value in entries.items():
            table[q] = value
        offsets[...] = product(0)

        def chunk(k, _):
            cut = pl.ds(pl.multiple_of(base + k * LANES, LANES), LANES)

            def px(q):
                return jnp.broadcast_to(table[q, pl.ds(k, 1), :], (SUBS, LANES))

            following = product(jnp.minimum(k + 1, CHUNKS - 1))
            gather_positions()
            total = squares = None
            for g in range(groups):
                at = slice(g * SUBS, (g + 1) * SUBS)
                visible = shadow_ref[at, cut].astype(jnp.float32)
                measured = [observed_ref[c, at, cut].astype(jnp.float32) for c in range(3)]
                sums, power_terms, square, cot = pair_terms(
                    px, [offsets[at, piece(b)] for b in range(BLOCKS)],
                    [power_wide[c, at, :] for c in range(3)], visible, measured,
                )
                total = sums if total is None else [a + b for a, b in zip(total, sums)]
                squares = square if squares is None else squares + square
                for b in range(BLOCKS):
                    spread_ref[at, piece(b)] = cot[b]
                for c in range(3):
                    power_sum[c, at, :] += power_terms[c]
            square_sum[...] += squares
            for q in range(SUMS):
                sums_ref[pl.ds((q * CHUNKS + k) * SUM_PITCH, SUBS), :] = total[q]
            frame_ref[...] = frame(k, 16)
            offsets[...] = following
            return 0

        arrive(step, 0, slice(4, 6))
        lax.fori_loop(0, CHUNKS, chunk, 0, unroll=UNROLL)
        grads = block_gradients(f, sums_ref)
        for q in range(ROWS):
            grads_ref[pl.ds(step * (CHUNKS * ROWS) + q, CHUNKS, stride=ROWS), :] = grads[q]
        return 0

    lax.fori_loop(0, steps, block, 0)

    gather_positions()
    wide = lax.broadcasted_iota(jnp.int32, (SUBS, LANES), 1)
    deep = lax.broadcasted_iota(jnp.int32, (SUBS, LANES), 0)
    lines = []
    for kind in range(2):
        spread = jnp.zeros((SUBS, LANES), jnp.float32)
        for c in range(3):
            for g in range(groups):
                at = slice(g * SUBS, (g + 1) * SUBS)
                if kind == 0:
                    line = jnp.sum(power_sum[c, at, :], axis=1, keepdims=True) / column(power_ref, c, g)
                else:
                    line = -pos_sum[at, c : c + 1] - 2.0 * column(pos_ref, c, g) * pos_sum[at, 4:5]
                spread = jnp.where(wide == deep + (g * SUBS + c * lights), line, spread)
        lines.append(jnp.sum(spread, axis=0, keepdims=True))
    first = lax.broadcasted_iota(jnp.int32, (1, LANES), 1)
    light_ref[0:1, :] = jnp.where(first == 3 * lights, whole(square_sum[...]), lines[0])
    light_ref[1:2, :] = lines[1]


def block_gradients(f, sums_ref):
    def summed(q):
        start = q * CHUNKS * SUM_PITCH
        parts = [sums_ref[pl.ds(start + i, CHUNKS, stride=SUM_PITCH), :] for i in range(SUBS)]
        while len(parts) > 1:
            parts = [a + b for a, b in zip(parts[::2], parts[1::2])]
        return parts[0]

    z = [summed(q) for q in range(SUMS)]
    vt, vb, vn = f["vt"], f["vb"], f["vn"]
    uv = z[SH] * f["rwv"] * f["rcv"]
    wv = -z[SH] * f["rwv"] * f["cv"] * f["vroot"]
    ax2, ay2, ix2, iy2 = f["ax2"], f["ay2"], f["ix2"], f["iy2"]
    pt, pb = uv * vt * ax2, uv * vb * ay2
    tau_x = (ay2 - 1.0) * z[V23] - z[TX] - (pb * vn + wv * vb)
    tau_y = (1.0 - ax2) * z[V13] + z[TY] + (pt * vn + wv * vt)
    tau_z = (iy2 * ax2 - 1.0) * z[V12] + (ay2 * ix2 - 1.0) * (z[U12] + pt * vb)
    turned = tau_x + f["inv"] * f["along"] * tau_z
    grads = [z[SD0 + c] * (0.5 / math.pi) for c in range(3)]
    grads += [z[SS0 + c] * f["lobe"] for c in range(3)]
    grads.append(z[V11] - (z[U11] + pt * vt) - z[SH])
    grads.append(z[V22] - (z[U22] + pb * vb) - z[SH])
    grads.append(f["kappa"] * (f["t_loc"][1] * tau_y - f["b_loc"][1] * turned))
    grads.append(f["kappa"] * (f["t_loc"][2] * tau_y - f["b_loc"][2] * turned))
    grads.append(tau_z * f["inv"] * f["inv"] * f["kappa"])
    grads.append((z[SF] - z[SH]) * f["inv_f1"])
    return grads


def local_gradients(observed, shadow, view_ids, points, frames, params, power, pos, cameras):
    lights, pixels = shadow.shape
    hbm = pl.BlockSpec(memory_space=pltpu.HBM)
    vmem = pl.BlockSpec(memory_space=pltpu.VMEM)
    return pl.pallas_call(
        gradient_kernel,
        in_specs=[pl.BlockSpec(memory_space=pltpu.SMEM)] + [hbm] * 6 + [vmem] * 2,
        out_specs=[vmem, vmem],
        out_shape=[
            jax.ShapeDtypeStruct((pixels // LANES * ROWS, LANES), jnp.float32),
            jax.ShapeDtypeStruct((2, LANES), jnp.float32),
        ],
        scratch_shapes=[
            pltpu.VMEM(observed.shape, observed.dtype),
            pltpu.VMEM(shadow.shape, jnp.int32),
            pltpu.VMEM((pixels // LANES, LANES), jnp.int32),
            pltpu.VMEM(points.shape, jnp.float32),
            pltpu.VMEM(frames.shape, jnp.float32),
            pltpu.VMEM(params.shape, jnp.float32),
            pltpu.VMEM((CHUNKS * RAW, LANES), jnp.float32),
            pltpu.VMEM((TABLE, CHUNKS, LANES), jnp.float32),
            pltpu.VMEM((SUMS * CHUNKS * SUM_PITCH, LANES), jnp.float32),
            pltpu.VMEM((lights, DEPTH), jnp.bfloat16),
            pltpu.VMEM((BLOCKS * CHUNKS * PITCH, LANES), jnp.float32),
            pltpu.VMEM((lights, BLOCKS * LANES), jnp.float32),
            pltpu.VMEM((lights, BLOCKS * LANES), jnp.float32),
            pltpu.VMEM((16, BLOCKS * LANES), jnp.bfloat16),
            pltpu.VMEM((3, lights, LANES), jnp.float32),
            pltpu.VMEM((3, lights, LANES), jnp.float32),
            pltpu.VMEM((lights, 16), jnp.float32),
            pltpu.VMEM((SUBS, LANES), jnp.float32),
            pltpu.SemaphoreType.DMA((2, 6)),
        ],
        compiler_params=pltpu.CompilerParams(vmem_limit_bytes=16 << 20),
        name="pair_gradients",
    )(
        *(
            pltpu.with_memory_space_constraint(x, pltpu.HBM)
            for x in (
                cameras, observed, shadow, view_ids.reshape(pixels // LANES, LANES),
                points, frames, params, power, pos,
            )
        )
    )


def share_kernel(mark, arrived_ref, light_ref, share_ref, spread_ref):
    parts, rows = arrived_ref.shape[:2]
    squares = jnp.zeros((SUBS, LANES), jnp.float32)
    for at in range(0, rows, SUBS):
        pieces = [arrived_ref[i, at : at + SUBS, :] for i in range(parts)]
        while len(pieces) > 1:
            pieces = [a + b for a, b in zip(pieces[::2], pieces[1::2])]
        share_ref[at : at + SUBS, :] = pieces[0]
        squares = squares + pieces[0] * pieces[0]
    lane = lax.broadcasted_iota(jnp.int32, (2, LANES), 1)
    deep = lax.broadcasted_iota(jnp.int32, (2, LANES), 0)
    tile = jnp.where((lane == mark) & (deep == 1), whole(squares), light_ref[...])
    for i in range(spread_ref.shape[0]):
        spread_ref[i] = tile


def join_kernel(mark, share_ref, light_parts_ref, out_ref, light_ref):
    tile = light_parts_ref[0]
    for i in range(1, light_parts_ref.shape[0]):
        tile = tile + light_parts_ref[i]
    light_ref[...] = tile
    lane = lax.broadcasted_iota(jnp.int32, (2, LANES), 1)
    light_sq = whole(jnp.where(lane < mark, tile * tile, 0.0))
    deep = lax.broadcasted_iota(jnp.int32, (SUBS, LANES), 0)
    wide = lax.broadcasted_iota(jnp.int32, (SUBS, LANES), 1)
    tail = jnp.where(wide == 0, light_sq, 0.0)
    tail = jnp.where(wide == 1, tile[0:1, mark : mark + 1], tail)
    tail = jnp.where(wide == 2, tile[1:2, mark : mark + 1], tail)
    tail = jnp.where(deep == 0, tail, 0.0)
    rows = share_ref.shape[0]
    for at in range(0, rows, SUBS):
        value = share_ref[at : at + SUBS, :]
        for i in range(out_ref.shape[0]):
            out_ref[i, at : at + SUBS, :] = value
    for i in range(out_ref.shape[0]):
        out_ref[i, rows : rows + SUBS, :] = tail


def step_kernel(
    pixel_total, light_total, gathered_ref, light_ref, params_ref, power_ref, pos_ref,
    new_params_ref, new_power_ref, new_pos_ref, loss_ref,
):
    parts, rows = gathered_ref.shape[0], gathered_ref.shape[1] - SUBS
    tail = gathered_ref[0, rows : rows + SUBS, :]
    for i in range(1, parts):
        tail = tail + gathered_ref[i, rows : rows + SUBS, :]
    light_scale = STRIDE * lax.rsqrt(tail[0:1, 0:1] / (6 * light_total) + EPS)
    pixel_scale = STRIDE * lax.rsqrt(tail[0:1, 2:3] / (ROWS * pixel_total) + EPS)
    loss_ref[...] = tail[0:1, 1:2] / (3.0 * light_total * pixel_total)
    lights = power_ref.shape[1]
    for c in range(3):
        cut = slice(c * lights, (c + 1) * lights)
        new_power_ref[c : c + 1, :] = power_ref[c : c + 1, :] - light_ref[0:1, cut] * light_scale
        new_pos_ref[c : c + 1, :] = pos_ref[c : c + 1, :] - light_ref[1:2, cut] * light_scale
    chunks = rows // ROWS
    for i in range(parts):
        for k in range(chunks):
            cut = slice((i * chunks + k) * LANES, (i * chunks + k + 1) * LANES)
            grad = gathered_ref[i, k * ROWS : (k + 1) * ROWS, :]
            new_params_ref[:, cut] = params_ref[:, cut] - grad * pixel_scale


def broadcast_exchange(x, axes):
    return lax.all_to_all(x, axes, split_axis=0, concat_axis=0, tiled=True)


def shards(observed, shadow, view_ids, points, frames, params, power, pos, cameras):
    lights, pixels = shadow.shape
    px_size, lt_size = lax.axis_size(PX), lax.axis_size(LT)
    grads, light_tile = local_gradients(
        observed, shadow, view_ids, points, frames, params, power, pos, cameras
    )
    share_rows = grads.shape[0] // lt_size
    mark = 3 * lights
    small = pltpu.CompilerParams(vmem_limit_bytes=8 << 20)
    arrived = broadcast_exchange(grads.reshape(lt_size, share_rows, LANES), LT)
    share, spread = pl.pallas_call(
        functools.partial(share_kernel, mark),
        out_shape=(
            jax.ShapeDtypeStruct((share_rows, LANES), jnp.float32),
            jax.ShapeDtypeStruct((px_size, 2, LANES), jnp.float32),
        ),
        compiler_params=small,
        name="share_sum",
    )(arrived, light_tile)
    light_parts = broadcast_exchange(spread, PX)
    joined, own_lights = pl.pallas_call(
        functools.partial(join_kernel, mark),
        out_shape=(
            jax.ShapeDtypeStruct((lt_size, share_rows + SUBS, LANES), jnp.float32),
            jax.ShapeDtypeStruct((2, LANES), jnp.float32),
        ),
        compiler_params=small,
        name="join",
    )(share, light_parts)
    gathered = broadcast_exchange(joined, LT)
    new_params, new_power, new_pos, loss = pl.pallas_call(
        functools.partial(step_kernel, pixels * px_size, lights * lt_size),
        out_shape=(
            jax.ShapeDtypeStruct(params.shape, jnp.float32),
            jax.ShapeDtypeStruct(power.shape, jnp.float32),
            jax.ShapeDtypeStruct(pos.shape, jnp.float32),
            jax.ShapeDtypeStruct((1, 1), jnp.float32),
        ),
        compiler_params=small,
        name="step",
    )(gathered, own_lights, params, power, pos)
    return new_params, new_power, new_pos, loss.reshape(())


def solution(mesh):
    torus = Mesh(mesh.devices.reshape(4, 4, 2, 8, 2), PX + LT)
    placed = (
        P(None, LT, PX),
        P(LT, PX),
        P(PX),
        P(None, PX),
        P(None, PX),
        P(None, PX),
        P(None, LT),
        P(None, LT),
        P(),
    )
    return jax.shard_map(
        shards,
        mesh=torus,
        in_specs=placed,
        out_specs=(P(None, PX), P(None, LT), P(None, LT), P()),
        check_vma=False,
    )
```

time: 79.2 us -> 78.1 us (0.986)
  Pallas kernels: 14.2 us -> 13.1 us
    pallas_call x1, Pallas kernels: 13 us -> 11.8 us  [local_gradients(): pl.pallas_call(gradient_kernel, in_specs=[pl.BlockSpec(memory_space=pltpu...]
where the time goes in v3:
time: 78.1 us; the launch traced here: 77.4 us
  blocking collectives  63.6 us (81%)
  Pallas kernels  13.1 us (17%)
    all_to_all x3, blocking collectives, broadcast_exchange(): return lax.all_to_all(x, axes, split_axis=0, concat_axis=0, tiled=True)  63.6 us
    pallas_call x1, Pallas kernels, local_gradients(): pl.pallas_call(gradient_kernel, in_specs=[pl.BlockSpec(memory_space=pltpu...  11.8 us

profile of v3, /device:TPU:1, one launch (start us, length us, event | category | flops | bytes accessed | tf_op | source)
XLA Modules:
  0.0 77.4 jit_solution(4756549211377067823)
XLA Ops:
  0.6 11.8 %pair_gradients.1 = (f32[768,128]{1,0:T(8,128)S(1)}, f32[2,128]{1,0:T(2,128)S(1)}) custom-call(f32[3,16]{1,0:T(4,128)} %camera_ref.1, bf16[3,32,8192]{2,1,0:T(8,128)(2,1)} %observed_hbm.1, s32[32,8192]{1,0:T(8,128)} %shadow_hbm.1, s32[64,128]{1,0:T(8,128)} %bitcast.4, f32[3,8192]{1,0:T(4,128)} %points_hbm.1, f32[2,8192]{1,0:T(2,128)} %frames_hbm.1, ...), custom_call_target="tpu_custom_call" | custom-call | tf_op jit(solution)/shard_map/pair_gradients/pallas_call | solution.py:398
  12.5 0.0 copy-start
  12.5 0.0 copy-start.1
  12.5 0.0 copy-start.2
  12.5 22.9 %all_to_all.15.arrived_ref = f32[16,48,128]{2,1,0:T(8,128)S(1)} all-to-all(f32[16,48,128]{2,1,0:T(8,128)S(1)} %bitcast.3), channel_id=1, replica_groups=mesh['px_0'=4,'px_1'=4,'px_2'=2,'lt_0'=8,'lt_1'=2] {'lt_0','lt_1'}, dimensions={0} | all-to-all | bytes 786432 | tf_op jit(solution)/shard_map/all_to_all | solution.py:503
  35.4 0.1 share_sum.1
  35.5 23.5 %all_to_all.16.light_parts_ref = f32[32,2,128]{2,1,0:T(2,128)S(1)} all-to-all(f32[32,2,128]{2,1,0:T(2,128)S(1)} %get-tuple-element.17), channel_id=1, replica_groups=mesh['px_0'=4,'px_1'=4,'px_2'=2,'lt_0'=8,'lt_1'=2] {'px_0','px_1','px_2'}, dimensions={0} | all-to-all | bytes 65536 | tf_op jit(solution)/shard_map/all_to_all | solution.py:503
  59.0 0.1 join.1
  59.2 17.3 %all_to_all.17.gathered_ref = f32[16,56,128]{2,1,0:T(8,128)S(1)} all-to-all(f32[16,56,128]{2,1,0:T(8,128)S(1)} %get-tuple-element.18), channel_id=1, replica_groups=mesh['px_0'=4,'px_1'=4,'px_2'=2,'lt_0'=8,'lt_1'=2] {'lt_0','lt_1'}, dimensions={0} | all-to-all | bytes 917504 | tf_op jit(solution)/shard_map/all_to_all | solution.py:503
  76.4 0.0 copy-done
  76.4 0.0 copy-done.1
  76.4 0.0 copy-done.2
  76.4 1.0 %step.1 = (f32[12,8192]{1,0:T(8,128)}, f32[3,32]{1,0:T(4,128)}, f32[3,32]{1,0:T(4,128)}, f32[1,1]{1,0:T(1,128)}) custom-call(f32[16,56,128]{2,1,0:T(8,128)S(1)} %all_to_all.17.gathered_ref, f32[2,128]{1,0:T(2,128)S(1)} %get-tuple-element.19.light_ref, f32[12,8192]{1,0:T(8,128)S(1)} %copy-done, f32[3,32]{1,0:T(4,128)S(1)} %copy-done.1, f32[3,32]{1,0:T(4,128)S(1)} %copy-done.2), custom_call_target="tpu_custom_call" | custom-call | tf_op jit(solution)/shard_map/step/pallas_call | solution.py:536
Async XLA Ops:
  12.5 63.9 %copy-start = (f32[12,8192]{1,0:T(8,128)S(1)}, f32[12,8192]{1,0:T(8,128)}, u32[]{:S(2)}) copy-start(f32[12,8192]{1,0:T(8,128)} %params_ref.1) | copy-start | bytes 1179652
  12.5 63.9 %copy-start.1 = (f32[3,32]{1,0:T(4,128)S(1)}, f32[3,32]{1,0:T(4,128)}, u32[]{:S(2)}) copy-start(f32[3,32]{1,0:T(4,128)} %power_ref.3) | copy-start | bytes 1156
  12.5 63.9 %copy-start.2 = (f32[3,32]{1,0:T(4,128)S(1)}, f32[3,32]{1,0:T(4,128)}, u32[]{:S(2)}) copy-start(f32[3,32]{1,0:T(4,128)} %pos_ref.3) | copy-start | bytes 1156

commit v4 on v3

--- a/solution.py
+++ b/solution.py
@@ -21,17 +21,18 @@
 BLOCK = 2048
 CHUNKS = BLOCK // LANES
 RAW = 25
-DEPTH = 32
-PITCH = 33
+DEPTH = 16
+PITCH = 17
 SUM_PITCH = 9
-UNROLL = 8
+UNROLL = 16
+PIECES = 4
 
 (VT, VB, VN, AX2, AY2, IX2, IY2, F0, F1, K5, KD0, KD1, KD2, KS0, KS1, KS2) = range(16)
 TABLE = 16
 (SD0, SD1, SD2, SS0, SS1, SS2, SF, SH, V11, V22, V12, V13, V23, U11, U22, U12, TX, TY) = range(18)
 SUMS = 18
-LEFT = (0, 0, 1, 1, 0, 2)
-RIGHT = (0, 1, 0, 1, 2, 0)
+LEFT = (0, 0, 1)
+RIGHT = (0, 1, 0)
 COMPS = 5
 BLOCKS = 5
 SQUARED = 3
@@ -161,17 +162,16 @@
     return x.astype(jnp.bfloat16).astype(jnp.float32)
 
 
-def split_three(x):
+def split_two(x):
     first = rounded(x)
-    second = rounded(x - first)
-    return [first, second, x - first - second]
+    return [first, x - first]
 
 
 def gradient_kernel(
     camera_ref, observed_hbm, shadow_hbm, ids_hbm, points_hbm, frames_hbm, params_hbm, power_ref, pos_ref,
     grads_ref, light_ref,
     observed_ref, shadow_ref, ids_ref, points_ref, frames_ref, params_ref,
-    raw, table, sums_ref, left, right, offsets, spread_ref, frame_ref, power_wide, power_sum, pos_sum,
+    raw, table, sums_ref, left, right, offsets, spread_ref, frames_packed, power_wide, power_sum, pos_sum,
     square_sum, sems,
 ):
     lights, pixels = shadow_hbm.shape
@@ -200,7 +200,7 @@
     pos_sum[...] = jnp.zeros_like(pos_sum)
     square_sum[...] = jnp.zeros_like(square_sum)
     spread_ref[...] = jnp.zeros_like(spread_ref)
-    frame_ref[...] = jnp.zeros_like(frame_ref)
+    frames_packed[...] = jnp.zeros_like(frames_packed)
     right[...] = jnp.zeros_like(right)
 
     def piece(b):
@@ -228,7 +228,7 @@
         for c in range(3):
             power_wide[c, at, :] = jnp.broadcast_to(column(power_ref, c, g), (SUBS, LANES))
         pos = [jnp.broadcast_to(column(pos_ref, c, g), (SUBS, DEPTH)) for c in range(3)]
-        splits = [split_three(x) for x in pos] + [[one, zero, zero], split_three(inner_three(pos, pos))]
+        splits = [split_two(x) for x in pos] + [[one, zero], split_two(inner_three(pos, pos))]
         tile = zero
         for i, part in enumerate(LEFT):
             for c in range(COMPS):
@@ -236,17 +236,16 @@
         tiles.append(tile)
     left[...] = jnp.concatenate(tiles, axis=0).astype(jnp.bfloat16)
 
-    def frame(k, depth):
-        return jnp.concatenate(
-            [right[pl.ds((b * CHUNKS + k) * PITCH, depth), :] for b in range(BLOCKS)], axis=1
+    def product(k):
+        frame = jnp.concatenate(
+            [right[pl.ds((b * CHUNKS + k) * PITCH, DEPTH), :] for b in range(BLOCKS)], axis=1
         ).astype(jnp.bfloat16)
-
-    def product(k):
-        return jnp.dot(left[...], frame(k, DEPTH), preferred_element_type=jnp.float32)
-
-    def gather_positions():
+        frames_packed[k] = frame
+        return jnp.dot(left[...], frame, preferred_element_type=jnp.float32)
+
+    def gather_positions(k):
         pos_sum[...] += lax.dot_general(
-            spread_ref[...].astype(jnp.bfloat16), frame_ref[...], (((1,), (1,)), ((), ())),
+            spread_ref[...].astype(jnp.bfloat16), frames_packed[k], (((1,), (1,)), ((), ())),
             preferred_element_type=jnp.float32,
         )
 
@@ -287,8 +286,7 @@
         columns.append([*f["view_dir"], -inner_three(point, f["view_dir"])])
         for b, column_of in enumerate(columns):
             for c, value in enumerate(column_of):
-                rest = value - rounded(value)
-                parts = [value, rest, rest - rounded(rest)]
+                parts = [value, value - rounded(value)]
                 for i, part in enumerate(RIGHT):
                     right[right_rows(b, i * COMPS + c), :] = parts[part]
         entries = {
@@ -310,7 +308,7 @@
                 return jnp.broadcast_to(table[q, pl.ds(k, 1), :], (SUBS, LANES))
 
             following = product(jnp.minimum(k + 1, CHUNKS - 1))
-            gather_positions()
+            gather_positions(jnp.where(k == 0, CHUNKS, k) - 1)
             total = squares = None
             for g in range(groups):
                 at = slice(g * SUBS, (g + 1) * SUBS)
@@ -329,7 +327,6 @@
             square_sum[...] += squares
             for q in range(SUMS):
                 sums_ref[pl.ds((q * CHUNKS + k) * SUM_PITCH, SUBS), :] = total[q]
-            frame_ref[...] = frame(k, 16)
             offsets[...] = following
             return 0
 
@@ -342,7 +339,7 @@
 
     lax.fori_loop(0, steps, block, 0)
 
-    gather_positions()
+    gather_positions(CHUNKS - 1)
     wide = lax.broadcasted_iota(jnp.int32, (SUBS, LANES), 1)
     deep = lax.broadcasted_iota(jnp.int32, (SUBS, LANES), 0)
     lines = []
@@ -417,7 +414,7 @@
             pltpu.VMEM((BLOCKS * CHUNKS * PITCH, LANES), jnp.float32),
             pltpu.VMEM((lights, BLOCKS * LANES), jnp.float32),
             pltpu.VMEM((lights, BLOCKS * LANES), jnp.float32),
-            pltpu.VMEM((16, BLOCKS * LANES), jnp.bfloat16),
+            pltpu.VMEM((CHUNKS, DEPTH, BLOCKS * LANES), jnp.bfloat16),
             pltpu.VMEM((3, lights, LANES), jnp.float32),
             pltpu.VMEM((3, lights, LANES), jnp.float32),
             pltpu.VMEM((lights, 16), jnp.float32),
@@ -477,26 +474,37 @@
 
 def step_kernel(
     pixel_total, light_total, gathered_ref, light_ref, params_ref, power_ref, pos_ref,
-    new_params_ref, new_power_ref, new_pos_ref, loss_ref,
+    new_params_hbm, new_power_ref, new_pos_ref, loss_ref, stepped, sems,
 ):
     parts, rows = gathered_ref.shape[0], gathered_ref.shape[1] - SUBS
     tail = gathered_ref[0, rows : rows + SUBS, :]
     for i in range(1, parts):
         tail = tail + gathered_ref[i, rows : rows + SUBS, :]
+    pixel_scale = STRIDE * lax.rsqrt(tail[0:1, 2:3] / (ROWS * pixel_total) + EPS)
+    pixel_scale = jnp.broadcast_to(pixel_scale, (ROWS, LANES))
+    chunks = rows // ROWS
+    each = parts // PIECES
+    copies = []
+    for piece in range(PIECES):
+        for i in range(piece * each, (piece + 1) * each):
+            for k in range(chunks):
+                cut = slice((i * chunks + k) * LANES, (i * chunks + k + 1) * LANES)
+                grad = gathered_ref[i, k * ROWS : (k + 1) * ROWS, :]
+                stepped[:, cut] = params_ref[:, cut] - grad * pixel_scale
+        span = slice(piece * each * chunks * LANES, (piece + 1) * each * chunks * LANES)
+        copies.append(
+            pltpu.make_async_copy(stepped.at[:, span], new_params_hbm.at[:, span], sems.at[piece])
+        )
+        copies[-1].start()
     light_scale = STRIDE * lax.rsqrt(tail[0:1, 0:1] / (6 * light_total) + EPS)
-    pixel_scale = STRIDE * lax.rsqrt(tail[0:1, 2:3] / (ROWS * pixel_total) + EPS)
     loss_ref[...] = tail[0:1, 1:2] / (3.0 * light_total * pixel_total)
     lights = power_ref.shape[1]
     for c in range(3):
         cut = slice(c * lights, (c + 1) * lights)
         new_power_ref[c : c + 1, :] = power_ref[c : c + 1, :] - light_ref[0:1, cut] * light_scale
         new_pos_ref[c : c + 1, :] = pos_ref[c : c + 1, :] - light_ref[1:2, cut] * light_scale
-    chunks = rows // ROWS
-    for i in range(parts):
-        for k in range(chunks):
-            cut = slice((i * chunks + k) * LANES, (i * chunks + k + 1) * LANES)
-            grad = gathered_ref[i, k * ROWS : (k + 1) * ROWS, :]
-            new_params_ref[:, cut] = params_ref[:, cut] - grad * pixel_scale
+    for copy in copies:
+        copy.wait()
 
 
 def broadcast_exchange(x, axes):
@@ -541,6 +549,11 @@
             jax.ShapeDtypeStruct(pos.shape, jnp.float32),
             jax.ShapeDtypeStruct((1, 1), jnp.float32),
         ),
+        out_specs=(pl.BlockSpec(memory_space=pltpu.HBM),) + (pl.BlockSpec(memory_space=pltpu.VMEM),) * 3,
+        scratch_shapes=[
+            pltpu.VMEM(params.shape, jnp.float32),
+            pltpu.SemaphoreType.DMA((PIECES,)),
+        ],
         compiler_params=small,
         name="step",
     )(gathered, own_lights, params, power, pos)

time: 78.1 us -> 78.4 us (level)
  no operation moved by 1% of the time
where the time goes in v4:
time: 78.4 us; the launch traced here: 77.6 us
  blocking collectives  63.6 us (81%)
  Pallas kernels  13.3 us (17%)
    all_to_all x3, blocking collectives, broadcast_exchange(): return lax.all_to_all(x, axes, split_axis=0, concat_axis=0, tiled=True)  63.6 us
    pallas_call x1, Pallas kernels, local_gradients(): pl.pallas_call(gradient_kernel, in_specs=[pl.BlockSpec(memory_space=pltpu...  11.5 us

profile of v4, /device:TPU:1, one launch (start us, length us, event | category | flops | bytes accessed | tf_op | source)
XLA Modules:
  0.0 77.6 jit_solution(1997929904307894205)
XLA Ops:
  0.6 11.5 %pair_gradients.1 = (f32[768,128]{1,0:T(8,128)S(1)}, f32[2,128]{1,0:T(2,128)S(1)}) custom-call(f32[3,16]{1,0:T(4,128)} %camera_ref.1, bf16[3,32,8192]{2,1,0:T(8,128)(2,1)} %observed_hbm.1, s32[32,8192]{1,0:T(8,128)} %shadow_hbm.1, s32[64,128]{1,0:T(8,128)} %bitcast.4, f32[3,8192]{1,0:T(4,128)} %points_hbm.1, f32[2,8192]{1,0:T(2,128)} %frames_hbm.1, ...), custom_call_target="tpu_custom_call" | custom-call | tf_op jit(solution)/shard_map/pair_gradients/pallas_call | solution.py:395
  12.1 0.0 copy-start
  12.1 0.0 copy-start.1
  12.2 0.0 copy-start.2
  12.2 22.9 %all_to_all.15.arrived_ref = f32[16,48,128]{2,1,0:T(8,128)S(1)} all-to-all(f32[16,48,128]{2,1,0:T(8,128)S(1)} %bitcast.3), channel_id=1, replica_groups=mesh['px_0'=4,'px_1'=4,'px_2'=2,'lt_0'=8,'lt_1'=2] {'lt_0','lt_1'}, dimensions={0} | all-to-all | bytes 786432 | tf_op jit(solution)/shard_map/all_to_all | solution.py:511
  35.0 0.1 share_sum.1
  35.2 23.5 %all_to_all.16.light_parts_ref = f32[32,2,128]{2,1,0:T(2,128)S(1)} all-to-all(f32[32,2,128]{2,1,0:T(2,128)S(1)} %get-tuple-element.17), channel_id=1, replica_groups=mesh['px_0'=4,'px_1'=4,'px_2'=2,'lt_0'=8,'lt_1'=2] {'px_0','px_1','px_2'}, dimensions={0} | all-to-all | bytes 65536 | tf_op jit(solution)/shard_map/all_to_all | solution.py:511
  58.6 0.1 join.1
  58.8 17.3 %all_to_all.17.gathered_ref = f32[16,56,128]{2,1,0:T(8,128)S(1)} all-to-all(f32[16,56,128]{2,1,0:T(8,128)S(1)} %get-tuple-element.18), channel_id=1, replica_groups=mesh['px_0'=4,'px_1'=4,'px_2'=2,'lt_0'=8,'lt_1'=2] {'lt_0','lt_1'}, dimensions={0} | all-to-all | bytes 917504 | tf_op jit(solution)/shard_map/all_to_all | solution.py:511
  76.1 0.0 copy-done
  76.1 0.0 copy-done.1
  76.1 0.0 copy-done.2
  76.1 1.5 %step.1 = (f32[12,8192]{1,0:T(8,128)}, f32[3,32]{1,0:T(4,128)}, f32[3,32]{1,0:T(4,128)}, f32[1,1]{1,0:T(1,128)}) custom-call(f32[16,56,128]{2,1,0:T(8,128)S(1)} %all_to_all.17.gathered_ref, f32[2,128]{1,0:T(2,128)S(1)} %get-tuple-element.19.light_ref, f32[12,8192]{1,0:T(8,128)S(1)} %copy-done, f32[3,32]{1,0:T(4,128)S(1)} %copy-done.1, f32[3,32]{1,0:T(4,128)S(1)} %copy-done.2), custom_call_target="tpu_custom_call" | custom-call | tf_op jit(solution)/shard_map/step/pallas_call | solution.py:544
Async XLA Ops:
  12.1 63.9 %copy-start = (f32[12,8192]{1,0:T(8,128)S(1)}, f32[12,8192]{1,0:T(8,128)}, u32[]{:S(2)}) copy-start(f32[12,8192]{1,0:T(8,128)} %params_ref.1) | copy-start | bytes 1179652
  12.1 63.9 %copy-start.1 = (f32[3,32]{1,0:T(4,128)S(1)}, f32[3,32]{1,0:T(4,128)}, u32[]{:S(2)}) copy-start(f32[3,32]{1,0:T(4,128)} %power_ref.3) | copy-start | bytes 1156
  12.2 63.9 %copy-start.2 = (f32[3,32]{1,0:T(4,128)S(1)}, f32[3,32]{1,0:T(4,128)}, u32[]{:S(2)}) copy-start(f32[3,32]{1,0:T(4,128)} %pos_ref.3) | copy-start | bytes 1156

commit v5 on v4

--- a/solution.py
+++ b/solution.py
@@ -11,6 +11,7 @@
 
 PX = ("px_0", "px_1", "px_2")
 LT = ("lt_0", "lt_1")
+SHARES = ("lt_1", "lt_0")
 
 SOFT = 0.01
 EPS = 1e-06
@@ -25,7 +26,6 @@
 PITCH = 17
 SUM_PITCH = 9
 UNROLL = 16
-PIECES = 4
 
 (VT, VB, VN, AX2, AY2, IX2, IY2, F0, F1, K5, KD0, KD1, KD2, KS0, KS1, KS2) = range(16)
 TABLE = 16
@@ -474,37 +474,26 @@
 
 def step_kernel(
     pixel_total, light_total, gathered_ref, light_ref, params_ref, power_ref, pos_ref,
-    new_params_hbm, new_power_ref, new_pos_ref, loss_ref, stepped, sems,
+    new_params_ref, new_power_ref, new_pos_ref, loss_ref,
 ):
     parts, rows = gathered_ref.shape[0], gathered_ref.shape[1] - SUBS
     tail = gathered_ref[0, rows : rows + SUBS, :]
     for i in range(1, parts):
         tail = tail + gathered_ref[i, rows : rows + SUBS, :]
+    light_scale = STRIDE * lax.rsqrt(tail[0:1, 0:1] / (6 * light_total) + EPS)
     pixel_scale = STRIDE * lax.rsqrt(tail[0:1, 2:3] / (ROWS * pixel_total) + EPS)
-    pixel_scale = jnp.broadcast_to(pixel_scale, (ROWS, LANES))
-    chunks = rows // ROWS
-    each = parts // PIECES
-    copies = []
-    for piece in range(PIECES):
-        for i in range(piece * each, (piece + 1) * each):
-            for k in range(chunks):
-                cut = slice((i * chunks + k) * LANES, (i * chunks + k + 1) * LANES)
-                grad = gathered_ref[i, k * ROWS : (k + 1) * ROWS, :]
-                stepped[:, cut] = params_ref[:, cut] - grad * pixel_scale
-        span = slice(piece * each * chunks * LANES, (piece + 1) * each * chunks * LANES)
-        copies.append(
-            pltpu.make_async_copy(stepped.at[:, span], new_params_hbm.at[:, span], sems.at[piece])
-        )
-        copies[-1].start()
-    light_scale = STRIDE * lax.rsqrt(tail[0:1, 0:1] / (6 * light_total) + EPS)
     loss_ref[...] = tail[0:1, 1:2] / (3.0 * light_total * pixel_total)
     lights = power_ref.shape[1]
     for c in range(3):
         cut = slice(c * lights, (c + 1) * lights)
         new_power_ref[c : c + 1, :] = power_ref[c : c + 1, :] - light_ref[0:1, cut] * light_scale
         new_pos_ref[c : c + 1, :] = pos_ref[c : c + 1, :] - light_ref[1:2, cut] * light_scale
-    for copy in copies:
-        copy.wait()
+    chunks = rows // ROWS
+    for i in range(parts):
+        for k in range(chunks):
+            cut = slice((i * chunks + k) * LANES, (i * chunks + k + 1) * LANES)
+            grad = gathered_ref[i, k * ROWS : (k + 1) * ROWS, :]
+            new_params_ref[:, cut] = params_ref[:, cut] - grad * pixel_scale
 
 
 def broadcast_exchange(x, axes):
@@ -520,7 +509,7 @@
     share_rows = grads.shape[0] // lt_size
     mark = 3 * lights
     small = pltpu.CompilerParams(vmem_limit_bytes=8 << 20)
-    arrived = broadcast_exchange(grads.reshape(lt_size, share_rows, LANES), LT)
+    arrived = broadcast_exchange(grads.reshape(lt_size, share_rows, LANES), SHARES)
     share, spread = pl.pallas_call(
         functools.partial(share_kernel, mark),
         out_shape=(
@@ -540,7 +529,7 @@
         compiler_params=small,
         name="join",
     )(share, light_parts)
-    gathered = broadcast_exchange(joined, LT)
+    gathered = broadcast_exchange(joined, SHARES)
     new_params, new_power, new_pos, loss = pl.pallas_call(
         functools.partial(step_kernel, pixels * px_size, lights * lt_size),
         out_shape=(
@@ -549,11 +538,6 @@
             jax.ShapeDtypeStruct(pos.shape, jnp.float32),
             jax.ShapeDtypeStruct((1, 1), jnp.float32),
         ),
-        out_specs=(pl.BlockSpec(memory_space=pltpu.HBM),) + (pl.BlockSpec(memory_space=pltpu.VMEM),) * 3,
-        scratch_shapes=[
-            pltpu.VMEM(params.shape, jnp.float32),
-            pltpu.SemaphoreType.DMA((PIECES,)),
-        ],
         compiler_params=small,
         name="step",
     )(gathered, own_lights, params, power, pos)

time: 78.4 us -> 76.3 us (0.973)
  the two profiles are of different devices: /device:TPU:1 before, /device:TPU:8 now
where the time goes in v5:
time: 76.3 us; the launch traced here: 76 us
  blocking collectives  62.6 us (82%)
  Pallas kernels  12.7 us (17%)
    all_to_all x3, blocking collectives, broadcast_exchange(): return lax.all_to_all(x, axes, split_axis=0, concat_axis=0, tiled=True)  62.6 us
    pallas_call x1, Pallas kernels, local_gradients(): pl.pallas_call(gradient_kernel, in_specs=[pl.BlockSpec(memory_space=pltpu...  11.5 us

profile of v5, /device:TPU:8, one launch (start us, length us, event | category | flops | bytes accessed | tf_op | source)
XLA Modules:
  0.0 76.0 jit_solution(13108483557307665627)
XLA Ops:
  0.6 11.5 %pair_gradients.1 = (f32[768,128]{1,0:T(8,128)S(1)}, f32[2,128]{1,0:T(2,128)S(1)}) custom-call(f32[3,16]{1,0:T(4,128)} %camera_ref.1, bf16[3,32,8192]{2,1,0:T(8,128)(2,1)} %observed_hbm.1, s32[32,8192]{1,0:T(8,128)} %shadow_hbm.1, s32[64,128]{1,0:T(8,128)} %bitcast.4, f32[3,8192]{1,0:T(4,128)} %points_hbm.1, f32[2,8192]{1,0:T(2,128)} %frames_hbm.1, ...), custom_call_target="tpu_custom_call" | custom-call | tf_op jit(solution)/shard_map/pair_gradients/pallas_call | solution.py:395
  12.1 0.0 copy-start
  12.1 0.0 copy-start.1
  12.2 0.0 copy-start.2
  12.2 21.7 %all_to_all.15.arrived_ref = f32[16,48,128]{2,1,0:T(8,128)S(1)} all-to-all(f32[16,48,128]{2,1,0:T(8,128)S(1)} %bitcast.3), channel_id=1, replica_groups=mesh['px_0'=4,'px_1'=4,'px_2'=2,'lt_0'=8,'lt_1'=2] {'lt_1','lt_0'}, dimensions={0} | all-to-all | bytes 786432 | tf_op jit(solution)/shard_map/all_to_all | solution.py:500
  33.9 0.1 share_sum.1
  34.0 21.9 %all_to_all.16.light_parts_ref = f32[32,2,128]{2,1,0:T(2,128)S(1)} all-to-all(f32[32,2,128]{2,1,0:T(2,128)S(1)} %get-tuple-element.17), channel_id=1, replica_groups=mesh['px_0'=4,'px_1'=4,'px_2'=2,'lt_0'=8,'lt_1'=2] {'px_0','px_1','px_2'}, dimensions={0} | all-to-all | bytes 65536 | tf_op jit(solution)/shard_map/all_to_all | solution.py:500
  55.9 0.1 join.1
  56.1 19.0 %all_to_all.17.gathered_ref = f32[16,56,128]{2,1,0:T(8,128)S(1)} all-to-all(f32[16,56,128]{2,1,0:T(8,128)S(1)} %get-tuple-element.18), channel_id=1, replica_groups=mesh['px_0'=4,'px_1'=4,'px_2'=2,'lt_0'=8,'lt_1'=2] {'lt_1','lt_0'}, dimensions={0} | all-to-all | bytes 917504 | tf_op jit(solution)/shard_map/all_to_all | solution.py:500
  75.0 0.0 copy-done
  75.0 0.0 copy-done.1
  75.0 0.0 copy-done.2
  75.0 1.0 %step.1 = (f32[12,8192]{1,0:T(8,128)}, f32[3,32]{1,0:T(4,128)}, f32[3,32]{1,0:T(4,128)}, f32[1,1]{1,0:T(1,128)}) custom-call(f32[16,56,128]{2,1,0:T(8,128)S(1)} %all_to_all.17.gathered_ref, f32[2,128]{1,0:T(2,128)S(1)} %get-tuple-element.19.light_ref, f32[12,8192]{1,0:T(8,128)S(1)} %copy-done, f32[3,32]{1,0:T(4,128)S(1)} %copy-done.1, f32[3,32]{1,0:T(4,128)S(1)} %copy-done.2), custom_call_target="tpu_custom_call" | custom-call | tf_op jit(solution)/shard_map/step/pallas_call | solution.py:533
Async XLA Ops:
  12.1 62.9 %copy-start = (f32[12,8192]{1,0:T(8,128)S(1)}, f32[12,8192]{1,0:T(8,128)}, u32[]{:S(2)}) copy-start(f32[12,8192]{1,0:T(8,128)} %params_ref.1) | copy-start | bytes 1179652
  12.1 62.9 %copy-start.1 = (f32[3,32]{1,0:T(4,128)S(1)}, f32[3,32]{1,0:T(4,128)}, u32[]{:S(2)}) copy-start(f32[3,32]{1,0:T(4,128)} %power_ref.3) | copy-start | bytes 1156
  12.2 62.9 %copy-start.2 = (f32[3,32]{1,0:T(4,128)S(1)}, f32[3,32]{1,0:T(4,128)}, u32[]{:S(2)}) copy-start(f32[3,32]{1,0:T(4,128)} %pos_ref.3) | copy-start | bytes 1156

commit v6 on v5

--- a/solution.py
+++ b/solution.py
@@ -10,8 +10,8 @@
 from jax.sharding import PartitionSpec as P
 
 PX = ("px_0", "px_1", "px_2")
-LT = ("lt_0", "lt_1")
-SHARES = ("lt_1", "lt_0")
+LT = ("y_2", "y_1", "y_0", "z_0")
+SHARES = ("z_0", "y_0", "y_1", "y_2")
 
 SOFT = 0.01
 EPS = 1e-06
@@ -545,7 +545,7 @@
 
 
 def solution(mesh):
-    torus = Mesh(mesh.devices.reshape(4, 4, 2, 8, 2), PX + LT)
+    torus = Mesh(mesh.devices.reshape(4, 4, 2, 2, 2, 2, 2), PX + LT)
     placed = (
         P(None, LT, PX),
         P(LT, PX),

time: 76.3 us -> 77.3 us (1.013)
  the two profiles are of different devices: /device:TPU:8 before, /device:TPU:1 now
where the time goes in v6:
time: 77.3 us; the launch traced here: 76.5 us
  blocking collectives  63 us (82%)
  Pallas kernels  12.7 us (16%)
    all_to_all x3, blocking collectives, broadcast_exchange(): return lax.all_to_all(x, axes, split_axis=0, concat_axis=0, tiled=True)  63 us
    pallas_call x1, Pallas kernels, local_gradients(): pl.pallas_call(gradient_kernel, in_specs=[pl.BlockSpec(memory_space=pltpu...  11.5 us

profile of v6, /device:TPU:1, one launch (start us, length us, event | category | flops | bytes accessed | tf_op | source)
XLA Modules:
  0.0 76.5 jit_solution(13896195114844432372)
XLA Ops:
  0.6 11.5 %pair_gradients.1 = (f32[768,128]{1,0:T(8,128)S(1)}, f32[2,128]{1,0:T(2,128)S(1)}) custom-call(f32[3,16]{1,0:T(4,128)} %camera_ref.1, bf16[3,32,8192]{2,1,0:T(8,128)(2,1)} %observed_hbm.1, s32[32,8192]{1,0:T(8,128)} %shadow_hbm.1, s32[64,128]{1,0:T(8,128)} %bitcast.4, f32[3,8192]{1,0:T(4,128)} %points_hbm.1, f32[2,8192]{1,0:T(2,128)} %frames_hbm.1, ...), custom_call_target="tpu_custom_call" | custom-call | tf_op jit(solution)/shard_map/pair_gradients/pallas_call | solution.py:395
  12.1 0.0 copy-start
  12.1 0.0 copy-start.1
  12.2 0.0 copy-start.2
  12.2 22.3 %all_to_all.15.arrived_ref = f32[16,48,128]{2,1,0:T(8,128)S(1)} all-to-all(f32[16,48,128]{2,1,0:T(8,128)S(1)} %bitcast.3), channel_id=1, replica_groups=mesh['px_0'=4,'px_1'=4,'px_2'=2,'y_2'=2,'y_1'=2,'y_0'=2,'z_0'=2] {'z_0',..., dimensions={0} | all-to-all | bytes 786432 | tf_op jit(solution)/shard_map/all_to_all | solution.py:500
  34.5 0.1 share_sum.1
  34.6 24.0 %all_to_all.16.light_parts_ref = f32[32,2,128]{2,1,0:T(2,128)S(1)} all-to-all(f32[32,2,128]{2,1,0:T(2,128)S(1)} %get-tuple-element.17), channel_id=1, replica_groups=mesh['px_0'=4,'px_1'=4,'px_2'=2,'y_2'=2,'y_1'=2,'y_0'=2,'z_0'=2] {'px_0'..., dimensions={0} | all-to-all | bytes 65536 | tf_op jit(solution)/shard_map/all_to_all | solution.py:500
  58.6 0.1 join.1
  58.7 16.7 %all_to_all.17.gathered_ref = f32[16,56,128]{2,1,0:T(8,128)S(1)} all-to-all(f32[16,56,128]{2,1,0:T(8,128)S(1)} %get-tuple-element.18), channel_id=1, replica_groups=mesh['px_0'=4,'px_1'=4,'px_2'=2,'y_2'=2,'y_1'=2,'y_0'=2,'z_0'=2] {'z_0',..., dimensions={0} | all-to-all | bytes 917504 | tf_op jit(solution)/shard_map/all_to_all | solution.py:500
  75.5 0.0 copy-done
  75.5 0.0 copy-done.1
  75.5 0.0 copy-done.2
  75.5 1.0 %step.1 = (f32[12,8192]{1,0:T(8,128)}, f32[3,32]{1,0:T(4,128)}, f32[3,32]{1,0:T(4,128)}, f32[1,1]{1,0:T(1,128)}) custom-call(f32[16,56,128]{2,1,0:T(8,128)S(1)} %all_to_all.17.gathered_ref, f32[2,128]{1,0:T(2,128)S(1)} %get-tuple-element.19.light_ref, f32[12,8192]{1,0:T(8,128)S(1)} %copy-done, f32[3,32]{1,0:T(4,128)S(1)} %copy-done.1, f32[3,32]{1,0:T(4,128)S(1)} %copy-done.2), custom_call_target="tpu_custom_call" | custom-call | tf_op jit(solution)/shard_map/step/pallas_call | solution.py:533
Async XLA Ops:
  12.1 63.3 %copy-start = (f32[12,8192]{1,0:T(8,128)S(1)}, f32[12,8192]{1,0:T(8,128)}, u32[]{:S(2)}) copy-start(f32[12,8192]{1,0:T(8,128)} %params_ref.1) | copy-start | bytes 1179652
  12.1 63.3 %copy-start.1 = (f32[3,32]{1,0:T(4,128)S(1)}, f32[3,32]{1,0:T(4,128)}, u32[]{:S(2)}) copy-start(f32[3,32]{1,0:T(4,128)} %power_ref.3) | copy-start | bytes 1156
  12.2 63.3 %copy-start.2 = (f32[3,32]{1,0:T(4,128)S(1)}, f32[3,32]{1,0:T(4,128)}, u32[]{:S(2)}) copy-start(f32[3,32]{1,0:T(4,128)} %pos_ref.3) | copy-start | bytes 1156

commit v7 on v5

--- a/solution.py
+++ b/solution.py
@@ -12,6 +12,7 @@
 PX = ("px_0", "px_1", "px_2")
 LT = ("lt_0", "lt_1")
 SHARES = ("lt_1", "lt_0")
+BLOCK_SUMS = ("px_2", "px_0", "px_1")
 
 SOFT = 0.01
 EPS = 1e-06
@@ -519,7 +520,7 @@
         compiler_params=small,
         name="share_sum",
     )(arrived, light_tile)
-    light_parts = broadcast_exchange(spread, PX)
+    light_parts = broadcast_exchange(spread, BLOCK_SUMS)
     joined, own_lights = pl.pallas_call(
         functools.partial(join_kernel, mark),
         out_shape=(

time: 76.3 us -> 75.8 us (level)
  no operation moved by 1% of the time
where the time goes in v7:
time: 75.8 us; the launch traced here: 75.6 us
  blocking collectives  62.1 us (82%)
  Pallas kernels  12.7 us (17%)
    all_to_all x3, blocking collectives, broadcast_exchange(): return lax.all_to_all(x, axes, split_axis=0, concat_axis=0, tiled=True)  62.1 us
    pallas_call x1, Pallas kernels, local_gradients(): pl.pallas_call(gradient_kernel, in_specs=[pl.BlockSpec(memory_space=pltpu...  11.5 us

profile of v7, /device:TPU:8, one launch (start us, length us, event | category | flops | bytes accessed | tf_op | source)
XLA Modules:
  0.0 75.6 jit_solution(183983985595739328)
XLA Ops:
  0.6 11.5 %pair_gradients.1 = (f32[768,128]{1,0:T(8,128)S(1)}, f32[2,128]{1,0:T(2,128)S(1)}) custom-call(f32[3,16]{1,0:T(4,128)} %camera_ref.1, bf16[3,32,8192]{2,1,0:T(8,128)(2,1)} %observed_hbm.1, s32[32,8192]{1,0:T(8,128)} %shadow_hbm.1, s32[64,128]{1,0:T(8,128)} %bitcast.4, f32[3,8192]{1,0:T(4,128)} %points_hbm.1, f32[2,8192]{1,0:T(2,128)} %frames_hbm.1, ...), custom_call_target="tpu_custom_call" | custom-call | tf_op jit(solution)/shard_map/pair_gradients/pallas_call | solution.py:396
  12.1 0.0 copy-start
  12.1 0.0 copy-start.1
  12.2 0.0 copy-start.2
  12.2 21.7 %all_to_all.15.arrived_ref = f32[16,48,128]{2,1,0:T(8,128)S(1)} all-to-all(f32[16,48,128]{2,1,0:T(8,128)S(1)} %bitcast.3), channel_id=1, replica_groups=mesh['px_0'=4,'px_1'=4,'px_2'=2,'lt_0'=8,'lt_1'=2] {'lt_1','lt_0'}, dimensions={0} | all-to-all | bytes 786432 | tf_op jit(solution)/shard_map/all_to_all | solution.py:501
  33.9 0.1 share_sum.1
  34.0 21.9 %all_to_all.16.light_parts_ref = f32[32,2,128]{2,1,0:T(2,128)S(1)} all-to-all(f32[32,2,128]{2,1,0:T(2,128)S(1)} %get-tuple-element.17), channel_id=1, replica_groups=mesh['px_0'=4,'px_1'=4,'px_2'=2,'lt_0'=8,'lt_1'=2] {'px_2','px_0','px_1'}, dimensions={0} | all-to-all | bytes 65536 | tf_op jit(solution)/shard_map/all_to_all | solution.py:501
  55.9 0.1 join.1
  56.1 18.5 %all_to_all.17.gathered_ref = f32[16,56,128]{2,1,0:T(8,128)S(1)} all-to-all(f32[16,56,128]{2,1,0:T(8,128)S(1)} %get-tuple-element.18), channel_id=1, replica_groups=mesh['px_0'=4,'px_1'=4,'px_2'=2,'lt_0'=8,'lt_1'=2] {'lt_1','lt_0'}, dimensions={0} | all-to-all | bytes 917504 | tf_op jit(solution)/shard_map/all_to_all | solution.py:501
  74.6 0.0 copy-done
  74.6 0.0 copy-done.1
  74.6 0.0 copy-done.2
  74.6 1.0 %step.1 = (f32[12,8192]{1,0:T(8,128)}, f32[3,32]{1,0:T(4,128)}, f32[3,32]{1,0:T(4,128)}, f32[1,1]{1,0:T(1,128)}) custom-call(f32[16,56,128]{2,1,0:T(8,128)S(1)} %all_to_all.17.gathered_ref, f32[2,128]{1,0:T(2,128)S(1)} %get-tuple-element.19.light_ref, f32[12,8192]{1,0:T(8,128)S(1)} %copy-done, f32[3,32]{1,0:T(4,128)S(1)} %copy-done.1, f32[3,32]{1,0:T(4,128)S(1)} %copy-done.2), custom_call_target="tpu_custom_call" | custom-call | tf_op jit(solution)/shard_map/step/pallas_call | solution.py:534
Async XLA Ops:
  12.1 62.5 %copy-start = (f32[12,8192]{1,0:T(8,128)S(1)}, f32[12,8192]{1,0:T(8,128)}, u32[]{:S(2)}) copy-start(f32[12,8192]{1,0:T(8,128)} %params_ref.1) | copy-start | bytes 1179652
  12.1 62.4 %copy-start.1 = (f32[3,32]{1,0:T(4,128)S(1)}, f32[3,32]{1,0:T(4,128)}, u32[]{:S(2)}) copy-start(f32[3,32]{1,0:T(4,128)} %power_ref.3) | copy-start | bytes 1156
  12.2 62.4 %copy-start.2 = (f32[3,32]{1,0:T(4,128)S(1)}, f32[3,32]{1,0:T(4,128)}, u32[]{:S(2)}) copy-start(f32[3,32]{1,0:T(4,128)} %pos_ref.3) | copy-start | bytes 1156

commit v8 on v7

--- a/solution.py
+++ b/solution.py
@@ -12,7 +12,7 @@
 PX = ("px_0", "px_1", "px_2")
 LT = ("lt_0", "lt_1")
 SHARES = ("lt_1", "lt_0")
-BLOCK_SUMS = ("px_2", "px_0", "px_1")
+BLOCK_SUMS = ("px_2", "px_1", "px_0")
 
 SOFT = 0.01
 EPS = 1e-06

time: 75.8 us -> 75.9 us (level)
  no operation moved by 1% of the time
where the time goes in v8:
time: 75.9 us; the launch traced here: 75.6 us
  blocking collectives  62.2 us (82%)
  Pallas kernels  12.7 us (17%)
    all_to_all x3, blocking collectives, broadcast_exchange(): return lax.all_to_all(x, axes, split_axis=0, concat_axis=0, tiled=True)  62.2 us
    pallas_call x1, Pallas kernels, local_gradients(): pl.pallas_call(gradient_kernel, in_specs=[pl.BlockSpec(memory_space=pltpu...  11.5 us

profile of v8, /device:TPU:8, one launch (start us, length us, event | category | flops | bytes accessed | tf_op | source)
XLA Modules:
  0.0 75.6 jit_solution(6149246898057491451)
XLA Ops:
  0.6 11.5 %pair_gradients.1 = (f32[768,128]{1,0:T(8,128)S(1)}, f32[2,128]{1,0:T(2,128)S(1)}) custom-call(f32[3,16]{1,0:T(4,128)} %camera_ref.1, bf16[3,32,8192]{2,1,0:T(8,128)(2,1)} %observed_hbm.1, s32[32,8192]{1,0:T(8,128)} %shadow_hbm.1, s32[64,128]{1,0:T(8,128)} %bitcast.4, f32[3,8192]{1,0:T(4,128)} %points_hbm.1, f32[2,8192]{1,0:T(2,128)} %frames_hbm.1, ...), custom_call_target="tpu_custom_call" | custom-call | tf_op jit(solution)/shard_map/pair_gradients/pallas_call | solution.py:396
  12.1 0.0 copy-start
  12.1 0.0 copy-start.1
  12.2 0.0 copy-start.2
  12.2 21.7 %all_to_all.15.arrived_ref = f32[16,48,128]{2,1,0:T(8,128)S(1)} all-to-all(f32[16,48,128]{2,1,0:T(8,128)S(1)} %bitcast.3), channel_id=1, replica_groups=mesh['px_0'=4,'px_1'=4,'px_2'=2,'lt_0'=8,'lt_1'=2] {'lt_1','lt_0'}, dimensions={0} | all-to-all | bytes 786432 | tf_op jit(solution)/shard_map/all_to_all | solution.py:501
  33.9 0.1 share_sum.1
  34.0 21.9 %all_to_all.16.light_parts_ref = f32[32,2,128]{2,1,0:T(2,128)S(1)} all-to-all(f32[32,2,128]{2,1,0:T(2,128)S(1)} %get-tuple-element.17), channel_id=1, replica_groups=mesh['px_0'=4,'px_1'=4,'px_2'=2,'lt_0'=8,'lt_1'=2] {'px_2','px_1','px_0'}, dimensions={0} | all-to-all | bytes 65536 | tf_op jit(solution)/shard_map/all_to_all | solution.py:501
  55.9 0.1 join.1
  56.0 18.6 %all_to_all.17.gathered_ref = f32[16,56,128]{2,1,0:T(8,128)S(1)} all-to-all(f32[16,56,128]{2,1,0:T(8,128)S(1)} %get-tuple-element.18), channel_id=1, replica_groups=mesh['px_0'=4,'px_1'=4,'px_2'=2,'lt_0'=8,'lt_1'=2] {'lt_1','lt_0'}, dimensions={0} | all-to-all | bytes 917504 | tf_op jit(solution)/shard_map/all_to_all | solution.py:501
  74.6 0.0 copy-done
  74.6 0.0 copy-done.1
  74.6 0.0 copy-done.2
  74.6 1.0 %step.1 = (f32[12,8192]{1,0:T(8,128)}, f32[3,32]{1,0:T(4,128)}, f32[3,32]{1,0:T(4,128)}, f32[1,1]{1,0:T(1,128)}) custom-call(f32[16,56,128]{2,1,0:T(8,128)S(1)} %all_to_all.17.gathered_ref, f32[2,128]{1,0:T(2,128)S(1)} %get-tuple-element.19.light_ref, f32[12,8192]{1,0:T(8,128)S(1)} %copy-done, f32[3,32]{1,0:T(4,128)S(1)} %copy-done.1, f32[3,32]{1,0:T(4,128)S(1)} %copy-done.2), custom_call_target="tpu_custom_call" | custom-call | tf_op jit(solution)/shard_map/step/pallas_call | solution.py:534
Async XLA Ops:
  12.1 62.5 %copy-start = (f32[12,8192]{1,0:T(8,128)S(1)}, f32[12,8192]{1,0:T(8,128)}, u32[]{:S(2)}) copy-start(f32[12,8192]{1,0:T(8,128)} %params_ref.1) | copy-start | bytes 1179652
  12.1 62.5 %copy-start.1 = (f32[3,32]{1,0:T(4,128)S(1)}, f32[3,32]{1,0:T(4,128)}, u32[]{:S(2)}) copy-start(f32[3,32]{1,0:T(4,128)} %power_ref.3) | copy-start | bytes 1156
  12.2 62.5 %copy-start.2 = (f32[3,32]{1,0:T(4,128)S(1)}, f32[3,32]{1,0:T(4,128)}, u32[]{:S(2)}) copy-start(f32[3,32]{1,0:T(4,128)} %pos_ref.3) | copy-start | bytes 1156
